TPU v7x, 32 devices: a whole 2x2x4 slice. The times are simulated.
32 devices in a mesh: grp: 2 (over y), seq: 4 (over z), head: 4 (over x, core).
Axes of the slice: x: 2, y: 2, z: 4, core: 2. Of those that a mesh axis runs over, the one named last changes fastest.
Arguments:
- lin_q: bfloat16 [1024, 2048], P(('grp', 'seq'), 'head'), parts along dimension 0, may hold values from -6 to 6
- lin_k: bfloat16 [1024, 2048], P(('grp', 'seq'), 'head'), parts along dimension 0, may hold values from -6 to 6
- lin_v: bfloat16 [1024, 4096], P(('grp', 'seq'), 'head'), parts along dimension 0, may hold values from -6 to 6
- conv_q: bfloat16 [4, 2048], P(None, 'head'), may hold values from -3 to 3
- conv_k: bfloat16 [4, 2048], P(None, 'head'), may hold values from -3 to 3
- conv_v: bfloat16 [4, 4096], P(None, 'head'), may hold values from -3 to 3
- lin_z: bfloat16 [1024, 4096], P(('grp', 'seq'), 'head'), parts along dimension 0, may hold values from -6 to 6
- beta_logit: float32 [1024, 32], P(('grp', 'seq'), 'head'), parts along dimension 0, may hold values from -7 to 2
- log_decay: float32 [1024, 32], P(('grp', 'seq'), 'head'), parts along dimension 0, may hold values from -1.1 to 0
- attn_query: bfloat16 [1024, 4096], P(('grp', 'seq'), 'head'), parts along dimension 0, may hold values from -6 to 6
- attn_gate: bfloat16 [1024, 4096], P(('grp', 'seq'), 'head'), parts along dimension 0, may hold values from -6 to 6
- attn_kv: bfloat16 [1024, 2, 2, 256], P(('grp', 'seq')), parts along dimension 0, may hold values from -6 to 6
- doc_lengths: int32 [10], P('grp'), parts along dimension 0, may hold values from 1 to 128, 512 in all
Outputs:
- delta_out: bfloat16 [1024, 4096], P(('grp', 'seq'), 'head'), parts along dimension 0
- attn_out: bfloat16 [1024, 4096], P(('grp', 'seq'), 'head'), parts along dimension 0
There are 2 independent parts, one for each index of `grp`. A program takes and returns all parts, laid end to end along the dimension named above; an argument that names none is the same for every part. Nothing has to cross between parts.
Inputs may be any that keep to these rules, and one draw needn't show every extreme that they name: `doc_lengths`: the 5 documents packed in order into the slab; their lengths sum to 512.
All inputs are finite; a program needn't handle non-finite values.
Results may differ from a plain program's by a relative error of at most 0.0037.
Values may be sent and summed in bfloat16 or wider, within the bound.
A program may use at most 192 MiB of HBM per device.

v0:
```python
import jax
import jax.numpy as jnp
from jax import lax
from jax.sharding import PartitionSpec as P

DK = 128
DV = 128
QKH = 16
VALUE_HEADS = 32
AQ = 16
KVH = 2
AD = 256
BLOCK = 64


EXACT_PRECISION = lax.Precision.HIGHEST
NEGATIVE = -1e30


def passed_along(value, axis, steps):
    count = lax.axis_size(axis)
    initial, last = (max(0, -steps), min(count, count - steps))
    return lax.ppermute(value, axis, [(source, source + steps) for source in range(initial, last)])


def prefix_2(value, axis, combine, identity):
    length, index = (lax.axis_size(axis), lax.axis_index(axis))
    everything = jax.tree.map(
        lambda part, kind: lax.all_gather(part.astype(kind), axis),
        value,
        (jnp.bfloat16, jnp.bfloat16),
    )
    start = jax.tree.map(
        lambda part, zero: jnp.broadcast_to(jnp.asarray(zero, part.dtype), part.shape),
        value,
        identity,
    )

    def step(k, before):
        reached = k < index
        new = combine(
            before, jax.tree.map(lambda part, own: part[k].astype(own.dtype), everything, value)
        )
        return jax.tree.map(lambda a, b: jnp.where(reached, a, b), new, before)

    return lax.fori_loop(0, length, step, start)


def segment_ids(positions, doc_lengths):
    offsets = jnp.cumsum(doc_lengths) - doc_lengths
    return jnp.sum((offsets[None, :] <= positions[:, None]).astype(jnp.int32), axis=1)


def start_flags(positions, doc_lengths):
    offsets = jnp.cumsum(doc_lengths) - doc_lengths
    return jnp.any(offsets[None, :] == positions[:, None], axis=1)


def causal_conv(values, margin, weights, positions, segment, doc_lengths):
    row_count = values.shape[0]
    tap_count = weights.shape[0]
    extended = jnp.concatenate([margin, values], axis=0).astype(jnp.float32)
    conv_sum = jnp.zeros(values.shape, jnp.float32)
    for tap_index in range(tap_count):
        source = positions - (tap_count - 1) + tap_index
        inside = (segment_ids(source, doc_lengths) == segment).astype(jnp.float32)
        conv_sum = (
            conv_sum
            + extended[tap_index : tap_index + row_count]
            * weights[tap_index].astype(jnp.float32)[None, :]
            * inside[:, None]
        )
    return jax.nn.silu(conv_sum)


def unit_heads(values, head_size):
    shaped = values.reshape(values.shape[0], -1, head_size)
    return shaped * lax.rsqrt(jnp.sum(shaped * shaped, axis=-1, keepdims=True) + 1e-06)


def compose(first_pair, second_pair):
    joined_map = jnp.einsum(
        "hij,hjk->hik", second_pair[0], first_pair[0], precision=EXACT_PRECISION
    )
    joined_shift = (
        jnp.einsum("hij,hjk->hik", second_pair[0], first_pair[1], precision=EXACT_PRECISION)
        + second_pair[1]
    )
    return (joined_map, joined_shift)


def unit_lower_inverse(lower_part, block_len):
    identity = jnp.eye(block_len, dtype=jnp.float32)
    power = -lower_part
    inverse = identity + power
    for _ in range(max(block_len - 1, 1).bit_length() - 1):
        power = jnp.einsum("nhij,nhjk->nhik", power, power, precision=EXACT_PRECISION)
        inverse = jnp.einsum(
            "nhij,nhjk->nhik", inverse, identity + power, precision=EXACT_PRECISION
        )
    return inverse


def delta_blocks(queries, keys_unit, values, beta_gate, log_rates, segment, starts):
    row_count, head_count, key_size = keys_unit.shape
    value_size = values.shape[2]
    block_len = BLOCK
    block_count = row_count // block_len

    def to_blocks(array):
        return jnp.swapaxes(array.reshape((block_count, block_len) + array.shape[1:]), 1, 2)

    query_blk = to_blocks(queries)
    key_blk = to_blocks(keys_unit)
    value_blk = to_blocks(values)
    beta_blk = to_blocks(beta_gate)
    cumulative = jnp.cumsum(to_blocks(log_rates), axis=-1)
    segment_blk = segment.reshape(block_count, block_len)
    fresh_count = jnp.cumsum(starts.reshape(block_count, block_len).astype(jnp.int32), axis=-1)
    later_row = lax.broadcasted_iota(jnp.int32, (block_len, block_len), 0)
    earlier_col = lax.broadcasted_iota(jnp.int32, (block_len, block_len), 1)
    visible = (later_row >= earlier_col)[None] & (
        segment_blk[:, :, None] == segment_blk[:, None, :]
    )
    visible = visible[:, None]
    spread = cumulative[..., :, None] - cumulative[..., None, :]
    decay_mat = jnp.where(visible, jnp.exp(jnp.where(visible, spread, 0.0)), 0.0)
    carried = jnp.where((fresh_count == 0)[:, None, :], jnp.exp(cumulative), 0.0)
    key_key = jnp.einsum("nhik,nhjk->nhij", key_blk, key_blk, precision=EXACT_PRECISION)
    strict = (later_row > earlier_col).astype(jnp.float32)
    lower_part = decay_mat * strict * key_key * beta_blk[..., None, :]
    inverse = unit_lower_inverse(lower_part, block_len)
    right_side = jnp.concatenate([value_blk, carried[..., None] * key_blk], axis=-1)
    solved = jnp.einsum("nhij,nhjc->nhic", inverse, right_side, precision=EXACT_PRECISION)
    moved_values = solved[..., :value_size]
    moved_keys = solved[..., value_size:]
    query_key = jnp.einsum("nhik,nhjk->nhij", query_blk, key_blk, precision=EXACT_PRECISION)
    attend = decay_mat * query_key * beta_blk[..., None, :]
    out_zero = jnp.einsum("nhij,nhjv->nhiv", attend, moved_values, precision=EXACT_PRECISION)
    reach_part = carried[..., None] * query_blk - jnp.einsum(
        "nhij,nhjk->nhik", attend, moved_keys, precision=EXACT_PRECISION
    )
    weighted = (beta_blk * decay_mat[..., block_len - 1, :])[..., None] * key_blk
    block_map = carried[..., block_len - 1][..., None, None] * jnp.eye(
        key_size, dtype=jnp.float32
    ) - jnp.einsum("nhjk,nhjl->nhkl", weighted, moved_keys, precision=EXACT_PRECISION)
    block_shift = jnp.einsum("nhjk,nhjv->nhkv", weighted, moved_values, precision=EXACT_PRECISION)

    def advance(prefix, current):
        return (compose(prefix, current), prefix)

    eye_heads = jnp.broadcast_to(
        jnp.eye(key_size, dtype=jnp.float32), (head_count, key_size, key_size)
    )
    zero_heads = jnp.zeros((head_count, key_size, value_size), jnp.float32)
    device_pair, prefixes = lax.scan(advance, (eye_heads, zero_heads), (block_map, block_shift))
    baseline_output = out_zero + jnp.einsum(
        "nhik,nhkv->nhiv", reach_part, prefixes[1], precision=EXACT_PRECISION
    )
    complete_reach = jnp.einsum(
        "nhik,nhkl->nhil", reach_part, prefixes[0], precision=EXACT_PRECISION
    )
    return (device_pair, baseline_output, complete_reach, eye_heads, zero_heads)


def shards(
    lin_q,
    lin_k,
    lin_v,
    conv_q,
    conv_k,
    conv_v,
    lin_z,
    beta_logit,
    log_decay,
    attn_query,
    attn_gate,
    attn_kv,
    doc_lengths,
):
    row_count = lin_q.shape[0]
    seq_index = lax.axis_index("seq")
    positions = seq_index * row_count + jnp.arange(row_count, dtype=jnp.int32)
    segment = segment_ids(positions, doc_lengths)
    starts = start_flags(positions, doc_lengths)
    rim_from = row_count - conv_q.shape[0] + 1
    rim_q, rim_k, rim_v = passed_along(
        (lin_q[rim_from:], lin_k[rim_from:], lin_v[rim_from:]), "seq", 1
    )
    queries = unit_heads(
        causal_conv(lin_q, rim_q, conv_q, positions, segment, doc_lengths), DK
    ) * DK ** (-0.5)
    keys_unit = unit_heads(causal_conv(lin_k, rim_k, conv_k, positions, segment, doc_lengths), DK)
    values = causal_conv(lin_v, rim_v, conv_v, positions, segment, doc_lengths).reshape(
        row_count, -1, DV
    )
    head_count = values.shape[1]
    queries = jnp.repeat(queries, VALUE_HEADS // QKH, axis=1)
    keys_unit = jnp.repeat(keys_unit, VALUE_HEADS // QKH, axis=1)
    beta_gate = jax.nn.sigmoid(beta_logit)
    device_pair, baseline_output, complete_reach, eye_heads, zero_heads = delta_blocks(
        queries, keys_unit, values, beta_gate, log_decay, segment, starts
    )
    arriving_input = prefix_2(
        (device_pair[0], device_pair[1]), "seq", compose, (eye_heads, zero_heads)
    )
    delta_output = baseline_output + jnp.einsum(
        "dpjt,ptw->dpjw", complete_reach, arriving_input[1], precision=EXACT_PRECISION
    )
    delta_output = jnp.swapaxes(delta_output, 1, 2).reshape(row_count, head_count, DV)
    inverse_rms = lax.rsqrt(jnp.mean(delta_output * delta_output, axis=-1, keepdims=True) + 1e-06)
    gate_z = jax.nn.silu(lin_z.astype(jnp.float32).reshape(row_count, head_count, DV))
    delta_out = (
        (delta_output * inverse_rms * gate_z)
        .astype(jnp.bfloat16)
        .reshape(row_count, head_count * DV)
    )
    aq_local = attn_query.shape[1] // AD
    query_heads = attn_query.reshape(row_count, aq_local, AD)
    kv_head = lax.axis_index("head") * aq_local // (AQ // KVH)
    own_pair = lax.dynamic_index_in_dim(attn_kv, kv_head, axis=2, keepdims=False)
    score_scale = AD ** (-0.5)

    def absorb(running, kv_piece, first_row):
        row_top, row_total, accum = running
        piece_rows = kv_piece.shape[0]
        key_pos = first_row + jnp.arange(piece_rows, dtype=jnp.int32)
        key_seg = segment_ids(key_pos, doc_lengths)
        allowed = (
            (key_pos[None, :] <= positions[:, None])
            & (key_seg[None, :] == segment[:, None])
            & (key_pos[None, :] >= 0)
        )
        scores = (
            jnp.einsum(
                "qhd,kd->hqk", query_heads, kv_piece[:, 0], preferred_element_type=jnp.float32
            )
            * score_scale
        )
        masked = jnp.where(allowed[None], scores, NEGATIVE)
        new_top = jnp.maximum(row_top, jnp.max(masked, axis=-1))
        weights_f = jnp.where(allowed[None], jnp.exp(masked - new_top[..., None]), 0.0)
        rescale = jnp.exp(row_top - new_top)
        row_total = row_total * rescale + jnp.sum(weights_f, axis=-1)
        accum = accum * rescale[..., None] + jnp.einsum(
            "hqk,kd->hqd",
            weights_f.astype(jnp.bfloat16),
            kv_piece[:, 1],
            preferred_element_type=jnp.float32,
        )
        return (new_top, row_total, accum)

    start_state = (
        jnp.full((aq_local, row_count), NEGATIVE, jnp.float32),
        jnp.zeros((aq_local, row_count), jnp.float32),
        jnp.zeros((aq_local, row_count, AD), jnp.float32),
    )
    running = absorb(start_state, own_pair, seq_index * row_count)

    def hop(hop_step, loop_state):
        loop_running, kv_piece = loop_state
        kv_piece = passed_along(kv_piece, "seq", 1)
        loop_running = absorb(loop_running, kv_piece, (seq_index - hop_step - 1) * row_count)
        return (loop_running, kv_piece)

    running, _ = lax.fori_loop(0, lax.axis_size("seq") // 4, hop, (running, own_pair))
    row_top, row_total, accum = running
    attended = jnp.swapaxes(accum / row_total[..., None], 0, 1).reshape(row_count, aq_local * AD)
    attn_out = (attended * jax.nn.sigmoid(attn_gate.astype(jnp.float32))).astype(jnp.bfloat16)
    return (delta_out, attn_out)


def solution(mesh):
    return jax.shard_map(
        shards,
        mesh=mesh,
        in_specs=(
            P(("grp", "seq"), "head"),
            P(("grp", "seq"), "head"),
            P(("grp", "seq"), "head"),
            P(None, "head"),
            P(None, "head"),
            P(None, "head"),
            P(("grp", "seq"), "head"),
            P(("grp", "seq"), "head"),
            P(("grp", "seq"), "head"),
            P(("grp", "seq"), "head"),
            P(("grp", "seq"), "head"),
            P(("grp", "seq"), None, None, None),
            P("grp"),
        ),
        out_specs=(P(("grp", "seq"), "head"), P(("grp", "seq"), "head")),
        check_vma=False,
    )
```

profile of v0, /device:TPU:0, one launch (start us, length us, event | category | flops | bytes accessed | tf_op | source)
XLA Modules:
  0.0 133.3 jit_solution(12013541830469223574)
XLA Ops:
  8.0 4.9 %collective-permute-start.1 = (bf16[3,512]{1,0:T(4,128)(2,1)S(1)}, bf16[3,512]{1,0:T(4,128)(2,1)S(1)}, u32[]{:S(2)}, u32[]{:S(2)}) collective-permute-start(bf16[3,512]{1,0:T(4,128)(2,1)S(1)} %slice.116), channel_id=1, source_target_pairs={{0,4},{4,8},{8,12},{1,5},{5,9},{9,13},{2,6},{6,10},{10,14},{3,7},{... | collective-permute-start | bytes 9224 | tf_op jit(solution)/shard_map/ppermute | solution.py:23
  13.6 3.5 %collective-permute-start = (bf16[3,512]{1,0:T(4,128)(2,1)S(1)}, bf16[3,512]{1,0:T(4,128)(2,1)S(1)}, u32[]{:S(2)}, u32[]{:S(2)}) collective-permute-start(bf16[3,512]{1,0:T(4,128)(2,1)S(1)} %slice.107), channel_id=1, source_target_pairs={{0,4},{4,8},{8,12},{1,5},{5,9},{9,13},{2,6},{6,10},{10,14},{3,7},{... | collective-permute-start | bytes 9224 | tf_op jit(solution)/shard_map/ppermute | solution.py:23
  17.8 3.5 %collective-permute-start.2 = (bf16[3,1024]{1,0:T(4,128)(2,1)S(1)}, bf16[3,1024]{1,0:T(4,128)(2,1)S(1)}, u32[]{:S(2)}, u32[]{:S(2)}) collective-permute-start(bf16[3,1024]{1,0:T(4,128)(2,1)S(1)} %slice.125), channel_id=1, source_target_pairs={{0,4},{4,8},{8,12},{1,5},{5,9},{9,13},{2,6},{6,10},{10,14},{3,7},{... | collective-permute-start | bytes 18440 | tf_op jit(solution)/shard_map/ppermute | solution.py:23
  22.3 2.6 %collective-permute-start.3 = (bf16[128,2,256]{2,0,1:T(8,128)(2,1)}, bf16[128,2,256]{2,0,1:T(8,128)(2,1)}, u32[]{:S(2)}, u32[]{:S(2)}) collective-permute-start(bf16[128,2,256]{2,0,1:T(8,128)(2,1)} %bitcast.190), channel_id=1, source_target_pairs={{0,4},{4,8},{8,12},{1,5},{5,9},{9,13},{2,6},{6,10},{10,14},{3,7},{... | collective-permute-start | bytes 393224 | tf_op jit(solution)/shard_map/while/body/eval_jaxpr/ppermute | solution.py:23
  44.5 3.2 %fusion.60 = f32[2,8,128,128]{3,2,1,0:T(8,128)} fusion(f32[2,8,64,256]{3,2,1,0:T(8,128)S(1)} %fusion.32, f32[2,64,8,128]{3,1,0,2:T(8,128)S(1)} %bitcast.209, f32[2,8,64]{2,1,0:T(8,128)S(1)} %fusion.115), kind=kOutput, calls=%fused_computation.90 | convolution fusion | flops 201457664 | bytes 2105344 | tf_op jit(solution)/shard_map/nhjk,nhjv->nhkv/dot_general | solution.py:147
  47.7 2.0 %convolution_subtract_fusion = f32[2,8,128,128]{3,2,1,0:T(8,128)S(1)} fusion(f32[128,128]{1,0:T(8,128)S(1)} %fusion.105, f32[2,8]{1,0:T(2,128)S(1)} %slice_reduce_fusion, f32[2,8,64,256]{3,2,1,0:T(8,128)S(1)} %fusion.32, f32[2,64,8,128]{3,1,0,2:T(8,128)S(1)} %bitcast.210, f32[2,8,64]{2,1,0:T(8,128)S(1)} %fusion.115), kind=kOutput, calls=%fused_computation.23 | convolution fusion | flops 201981952 | bytes 2171904 | tf_op jit(solution)/shard_map/nhjk,nhjl->nhkl/dot_general | solution.py:146
  49.8 9.6 %while.10 = (s32[]{:T(128)}, f32[8,128,128]{2,1,0:T(8,128)S(1)}, f32[8,128,128]{2,1,0:T(8,128)S(1)}, f32[2,8,128,128]{3,2,1,0:T(8,128)}, f32[2,8,128,128]{3,2,1,...) while((s32[]{:T(128)}, f32[8,128,128]{2,1,0:T(8,128)S(1)}, ...), condition=%wide.region_11.12_spmd.clone, body=%wide.region_10.11_spmd.clone.sunk | while | flops 403046400 | bytes 28837632 | solution.py:156
  49.9 1.1 copy-done.6
  51.4 1.1 copy-done.1
  54.7 1.1 copy-done.6
  61.0 2.4 %fusion.118 = (f32[4,128]{1,0:T(4,128)}, f32[4,128,128]{1,2,0:T(8,128)}) fusion(bf16[16,4,8,256]{3,2,1,0:T(8,128)(2,1)S(1)} %bitcast.238, bf16[128,2,256]{2,0,1:T(8,128)(2,1)} %bitcast.190, pred[128,128]{0,1:T(8,128)(4,1)S(1)} %get-tuple-element.266), kind=kOutput, calls=%fused_computation.220 | convolution fusion | flops 33750528 | bytes 608256 | tf_op jit(solution)/shard_map/qhd,kd->hqk/dot_general | solution.py:235
  68.3 2.3 %fusion.125 = f32[2,8,64,128]{3,2,1,0:T(8,128)S(1)} fusion(f32[2,8,64,128]{3,2,1,0:T(8,128)S(1)} %convolution_subtract_fusion.1, f32[2,8,128,128]{3,2,1,0:T(8,128)} %get-tuple-element.173), kind=kOutput, calls=%fused_computation.227 | convolution fusion | flops 201326592 | bytes 2097152 | tf_op jit(solution)/shard_map/nhik,nhkl->nhil/dot_general | solution.py:160
  70.6 1.1 fusion.119
  72.6 1.1 fusion.26
  73.7 1.1 fusion.27
  75.2 1.8 %multiply_convert_fusion = bf16[128,1024]{1,0:T(8,128)(2,1)} fusion(f32[128,1024]{1,0:T(8,128)S(1)} %copy.95, bf16[128,1024]{1,0:T(8,128)(2,1)} %param.27), kind=kLoop, calls=%fused_computation.76 | loop fusion | flops 786432 | bytes 1048576 | tf_op jit(solution)/shard_map/convert_element_type | solution.py:269
  77.0 9.4 %all-gather.5.cloned.1.call-done = bf16[32,128,128]{2,1,0:T(8,128)(2,1)} async-done(((bf16[8,128,128]{2,1,0:T(8,128)(2,1)}), bf16[32,128,128]{2,1,0:T(8,128)(2,1)}) %all-gather.5.cloned.1.call-update) | async-done | bytes 1048592 | tf_op jit(solution)/shard_map/all_gather | solution.py:29
  86.4 29.0 %all-gather.7.cloned.1.call-done = bf16[32,128,128]{2,1,0:T(8,128)(2,1)} async-done(((bf16[8,128,128]{2,1,0:T(8,128)(2,1)}), bf16[32,128,128]{2,1,0:T(8,128)(2,1)}) %all-gather.7.cloned.1.call-update) | async-done | bytes 1048592 | tf_op jit(solution)/shard_map/all_gather | solution.py:29
  115.4 6.3 %while.40 = (s32[]{:T(128)}, f32[8,128,128]{2,1,0:T(8,128)S(1)}, s32[]{:T(128)}, bf16[4,8,128,128]{3,2,1,0:T(8,128)(2,1)}, bf16[4,8,128,128]{3,2,1,0:T(8,128)(2,1)}, /*index=5*/s32[]{:T(128)}, s32[]{:T(128)}) while((s32[]{:T(128)}, f32[8,128,128]{2,1,0:T(8,128)S(1)}, s32[]{:T(128)}, bf16[4,8,128,128]{3,2,1,0:T(8,128)(2,1)}, ...), condition=%wide.region_13.14_spmd.clone, body=%wide.region_12.13_spmd.clone.sunk | while | flops 201981952 | bytes 3148391 | solution.py:46
  115.5 1.5 %fusion.165 = f32[8,128,128]{2,1,0:T(8,128)S(1)} fusion(f32[8,128,128]{2,1,0:T(8,128)S(1)} %copy.185, bf16[4,8,128,128]{3,2,1,0:T(8,128)(2,1)} %get-tuple-element.406, s32[]{:T(128)S(6)} %copy.176, bf16[4,8,128,128]{3,2,1,0:T(8,128)(2,1)} %get-tuple-element.405, pred[]{:T(512)S(6)} %compare.9, pred[]{:T(512)S(6)} %lt.33), kind=kOutput, calls=%fused_computation.15.clone.1 | convolution fusion | flops 201981952 | bytes 2099712 | tf_op jit(solution)/shard_map/while/body/eval_jaxpr/hij,hjk->hik/dot_general | solution.py:86
  117.0 1.5 %fusion.165 = f32[8,128,128]{2,1,0:T(8,128)S(1)} fusion(f32[8,128,128]{2,1,0:T(8,128)S(1)} %copy.185, bf16[4,8,128,128]{3,2,1,0:T(8,128)(2,1)} %get-tuple-element.406, s32[]{:T(128)S(6)} %copy.176, bf16[4,8,128,128]{3,2,1,0:T(8,128)(2,1)} %get-tuple-element.405, pred[]{:T(512)S(6)} %compare.9, pred[]{:T(512)S(6)} %lt.33), kind=kOutput, calls=%fused_computation.15.clone.1 | convolution fusion | flops 201981952 | bytes 2099712 | tf_op jit(solution)/shard_map/while/body/eval_jaxpr/hij,hjk->hik/dot_general | solution.py:86
  118.6 1.5 %fusion.165 = f32[8,128,128]{2,1,0:T(8,128)S(1)} fusion(f32[8,128,128]{2,1,0:T(8,128)S(1)} %copy.185, bf16[4,8,128,128]{3,2,1,0:T(8,128)(2,1)} %get-tuple-element.406, s32[]{:T(128)S(6)} %copy.176, bf16[4,8,128,128]{3,2,1,0:T(8,128)(2,1)} %get-tuple-element.405, pred[]{:T(512)S(6)} %compare.9, pred[]{:T(512)S(6)} %lt.33), kind=kOutput, calls=%fused_computation.15.clone.1 | convolution fusion | flops 201981952 | bytes 2099712 | tf_op jit(solution)/shard_map/while/body/eval_jaxpr/hij,hjk->hik/dot_general | solution.py:86
  120.2 1.5 %fusion.165 = f32[8,128,128]{2,1,0:T(8,128)S(1)} fusion(f32[8,128,128]{2,1,0:T(8,128)S(1)} %copy.185, bf16[4,8,128,128]{3,2,1,0:T(8,128)(2,1)} %get-tuple-element.406, s32[]{:T(128)S(6)} %copy.176, bf16[4,8,128,128]{3,2,1,0:T(8,128)(2,1)} %get-tuple-element.405, pred[]{:T(512)S(6)} %compare.9, pred[]{:T(512)S(6)} %lt.33), kind=kOutput, calls=%fused_computation.15.clone.1 | convolution fusion | flops 201981952 | bytes 2099712 | tf_op jit(solution)/shard_map/while/body/eval_jaxpr/hij,hjk->hik/dot_general | solution.py:86
  122.9 1.1 multiply_reduce_fusion
  (180 shorter events, 39.8 us)
Async XLA Ops:
  7.2 14.1 %copy-start = (bf16[128,2,2,256]{3,2,1,0:T(2,128)(2,1)S(1)}, bf16[128,2,2,256]{3,2,1,0:T(2,128)(2,1)}, u32[]{:S(2)}) copy-start(bf16[128,2,2,256]{3,2,1,0:T(2,128)(2,1)} %param.28) | copy-start | bytes 786436
  7.2 79.2 %all-gather.5.cloned.1.call-start = ((), (), s32[]{:S(2)}) async-start(), calls=%async_computation | async-start | bytes 1310720 | tf_op jit(solution)/shard_map/all_gather | solution.py:29
  8.0 23.7 %collective-permute-start.1 = (bf16[3,512]{1,0:T(4,128)(2,1)S(1)}, bf16[3,512]{1,0:T(4,128)(2,1)S(1)}, u32[]{:S(2)}, u32[]{:S(2)}) collective-permute-start(bf16[3,512]{1,0:T(4,128)(2,1)S(1)} %slice.116), channel_id=1, source_target_pairs={{0,4},{4,8},{8,12},{1,5},{5,9},{9,13},{2,6},{6,10},{10,14},{3,7},{... | collective-permute-start | bytes 9224 | tf_op jit(solution)/shard_map/ppermute | solution.py:23
  13.6 18.0 %collective-permute-start = (bf16[3,512]{1,0:T(4,128)(2,1)S(1)}, bf16[3,512]{1,0:T(4,128)(2,1)S(1)}, u32[]{:S(2)}, u32[]{:S(2)}) collective-permute-start(bf16[3,512]{1,0:T(4,128)(2,1)S(1)} %slice.107), channel_id=1, source_target_pairs={{0,4},{4,8},{8,12},{1,5},{5,9},{9,13},{2,6},{6,10},{10,14},{3,7},{... | collective-permute-start | bytes 9224 | tf_op jit(solution)/shard_map/ppermute | solution.py:23
  17.8 24.2 %collective-permute-start.2 = (bf16[3,1024]{1,0:T(4,128)(2,1)S(1)}, bf16[3,1024]{1,0:T(4,128)(2,1)S(1)}, u32[]{:S(2)}, u32[]{:S(2)}) collective-permute-start(bf16[3,1024]{1,0:T(4,128)(2,1)S(1)} %slice.125), channel_id=1, source_target_pairs={{0,4},{4,8},{8,12},{1,5},{5,9},{9,13},{2,6},{6,10},{10,14},{3,7},{... | collective-permute-start | bytes 18440 | tf_op jit(solution)/shard_map/ppermute | solution.py:23
  22.3 48.3 %collective-permute-start.3 = (bf16[128,2,256]{2,0,1:T(8,128)(2,1)}, bf16[128,2,256]{2,0,1:T(8,128)(2,1)}, u32[]{:S(2)}, u32[]{:S(2)}) collective-permute-start(bf16[128,2,256]{2,0,1:T(8,128)(2,1)} %bitcast.190), channel_id=1, source_target_pairs={{0,4},{4,8},{8,12},{1,5},{5,9},{9,13},{2,6},{6,10},{10,14},{3,7},{... | collective-permute-start | bytes 393224 | tf_op jit(solution)/shard_map/while/body/eval_jaxpr/ppermute | solution.py:23
  31.5 2.7 %copy-start.18 = (f32[2,64,8]{1,2,0:T(8,128)}, f32[2,64,8]{1,2,0:T(8,128)S(1)}, u32[]{:S(2)}) copy-start(f32[2,64,8]{1,2,0:T(8,128)S(1)} %copy.155) | copy-start | bytes 12292
  44.5 3.2 %copy-start.2 = (f32[2,8,64,256]{3,2,1,0:T(8,128)}, f32[2,8,64,256]{3,2,1,0:T(8,128)S(1)}, u32[]{:S(2)}) copy-start(f32[2,8,64,256]{3,2,1,0:T(8,128)S(1)} %fusion.32) | copy-start | bytes 3145732
  49.8 1.2 copy-start.6
  49.8 1.5 %copy-start.9 = (f32[2,8,128,128]{3,2,1,0:T(8,128)S(1)}, f32[2,8,128,128]{3,2,1,0:T(8,128)}, u32[]{:S(2)}) copy-start(f32[2,8,128,128]{3,2,1,0:T(8,128)} %get-tuple-element.373) | copy-start | bytes 3145732 | tf_op jit(solution)/shard_map/while
  51.3 1.2 copy-start.1
  52.5 1.3 copy-start.10
  54.6 1.2 copy-start.6
  54.6 1.5 %copy-start.9 = (f32[2,8,128,128]{3,2,1,0:T(8,128)S(1)}, f32[2,8,128,128]{3,2,1,0:T(8,128)}, u32[]{:S(2)}) copy-start(f32[2,8,128,128]{3,2,1,0:T(8,128)} %get-tuple-element.373) | copy-start | bytes 3145732 | tf_op jit(solution)/shard_map/while
  56.1 1.2 copy-start.1
  57.3 1.3 copy-start.10
  60.1 55.3 %all-gather.7.cloned.1.call-start = ((), (), s32[]{:S(2)}) async-start(), calls=%async_computation.1 | async-start | bytes 1310720 | tf_op jit(solution)/shard_map/all_gather | solution.py:29
  61.0 2.4 %copy-start.12 = (f32[128,512]{1,0:T(8,128)S(1)}, f32[128,512]{1,0:T(8,128)}, u32[]{:S(2)}) copy-start(f32[128,512]{1,0:T(8,128)} %get-tuple-element.265) | copy-start | bytes 786436
  64.1 1.6 %copy-start.4 = (f32[128,4,2,128]{3,0,2,1:T(8,128)}, f32[128,4,2,128]{3,0,2,1:T(8,128)S(1)}, u32[]{:S(2)}) copy-start(f32[128,4,2,128]{3,0,2,1:T(8,128)S(1)} %broadcast_in_dim.88) | copy-start | bytes 1572868
  64.7 1.8 %copy-start.3 = (f32[2,8,64,256]{3,2,1,0:T(8,128)S(1)}, f32[2,8,64,256]{3,2,1,0:T(8,128)}, u32[]{:S(2)}) copy-start(f32[2,8,64,256]{3,2,1,0:T(8,128)} %copy-done.2) | copy-start | bytes 3145732
  68.2 2.3 %copy-start.17 = (pred[128,128]{0,1:T(8,128)(4,1)S(1)}, pred[128,128]{0,1:T(8,128)(4,1)}, u32[]{:S(2)}) copy-start(pred[128,128]{0,1:T(8,128)(4,1)} %get-tuple-element.267) | copy-start | bytes 49156
  68.2 2.3 %copy-start.27 = (bf16[128,1024]{1,0:T(8,128)(2,1)S(1)}, bf16[128,1024]{1,0:T(8,128)(2,1)}, u32[]{:S(2)}) copy-start(bf16[128,1024]{1,0:T(8,128)(2,1)} %param.26) | copy-start | bytes 786436
  70.6 1.8 %copy-start.11 = (f32[4,128,128]{1,2,0:T(8,128)S(1)}, f32[4,128,128]{1,2,0:T(8,128)}, u32[]{:S(2)}) copy-start(f32[4,128,128]{1,2,0:T(8,128)} %get-tuple-element.274) | copy-start | bytes 786436
  121.7 1.2 copy-start.8
  (16 other events, 13.3 us)
Sparse Core Ops, SparseCore 0:
  60.2 26.1 all-gather.4
  88.0 27.4 all-gather.6
where the time goes:
time: 134 us; the launch traced here: 133 us
  waiting for transfers between devices  38.4 us (29%)
  matrix products  34.5 us (26%)
  local copies, waits for them, and re-layouts  21.2 us (16%)
  between operations  14.7 us (11%)
  starting transfers between devices  14.5 us (11%)
  other arithmetic  9.61 us (7%)
    all_gather x2, waiting for transfers between devices, prefix_2(): lax.all_gather(part.astype(kind), axis)  38.4 us
    ppermute x4, starting transfers between devices, passed_along(): lax.ppermute(value, axis, [(source, source + steps) for source in range(i...  14.4 us
    unnamed x49, local copies, waits for them, and re-layouts  9.44 us
    dot_general x6, matrix products, compose(): jnp.einsum('hij,hjk->hik', second_pair[0], first_pair[1], precision=EXACT...  7.33 us
    while x28, local copies, waits for them, and re-layouts  6.73 us
    dot_general x2, matrix products, absorb(): jnp.einsum('qhd,kd->hqk', query_heads, kv_piece[:, 0], preferred_element_...  3.54 us
    dot_general x5, matrix products, unit_lower_inverse(): jnp.einsum('nhij,nhjk->nhik', inverse, identity + power, precision=EXACT_...  3.28 us
    dot_general x5, matrix products, unit_lower_inverse(): jnp.einsum('nhij,nhjk->nhik', power, power, precision=EXACT_PRECISION)  3.22 us
  transfers between devices with their start and end apart: 6, of which 2 were waited for; matrix products, arithmetic and copies ran while one was open for 29% of the time, Pallas kernels for 0%

commit v1 on v0

--- a/solution.py
+++ b/solution.py
@@ -1,6 +1,10 @@
+import functools
+
 import jax
 import jax.numpy as jnp
 from jax import lax
+from jax.experimental import pallas as pl
+from jax.experimental.pallas import tpu as pltpu
 from jax.sharding import PartitionSpec as P
 
 DK = 128
@@ -270,9 +274,361 @@
     return (delta_out, attn_out)
 
 
+BF = jnp.bfloat16
+F32 = jnp.float32
+LANES = 128
+GROUPS = 2
+
+
+def mm(a, b, transposed=False):
+    contract = ((1,), (1,)) if transposed else ((1,), (0,))
+    return lax.dot_general(a, b, (contract, ((), ())), preferred_element_type=F32)
+
+
+def halves(x):
+    high = x.astype(BF)
+    return high, (x - high.astype(F32)).astype(BF)
+
+
+def lhs3(x):
+    high, low = halves(x)
+    return jnp.concatenate([high, low, high], axis=1)
+
+
+def rhs3(x):
+    high, low = halves(x)
+    return jnp.concatenate([high, high, low], axis=0)
+
+
+def fused_kernel(
+    count,
+    doc_ref,
+    lin_q,
+    lin_k,
+    lin_v,
+    conv_q,
+    conv_k,
+    conv_v,
+    lin_z,
+    beta_logit,
+    log_decay,
+    attn_query,
+    attn_gate,
+    kv_own,
+    delta_out,
+    attn_out,
+    rim_q,
+    rim_k,
+    rim_v,
+    kv_before,
+    state_out,
+    state_in,
+    spread_q,
+    spread_k,
+    spread_v,
+    packed,
+    local_out,
+    reach_out,
+    send_sem,
+    recv_sem,
+):
+    rows = lin_q.shape[0]
+    heads = lin_v.shape[1] // DV
+    shared = heads // (lin_k.shape[1] // DK)
+    docs = doc_ref.shape[0]
+    rim = rim_q.shape[0]
+    index = lax.axis_index("seq")
+    barrier = pltpu.get_barrier_semaphore()
+
+    def transfer(source, target, slot):
+        return pltpu.make_async_remote_copy(
+            src_ref=source,
+            dst_ref=target,
+            send_sem=send_sem.at[slot],
+            recv_sem=recv_sem.at[slot],
+            device_id={"seq": index + 1},
+            device_id_type=pl.DeviceIdType.MESH,
+        )
+
+    tail = pl.ds(rows - rim, rim)
+    early = [
+        transfer(lin_k.at[tail, :], rim_k, 0),
+        transfer(lin_v.at[tail, :], rim_v, 1),
+        transfer(lin_q.at[tail, :], rim_q, 2),
+        transfer(kv_own, kv_before, 3),
+    ]
+    per_group = heads // GROUPS
+    states = [
+        transfer(
+            state_out.at[pl.ds(g * per_group, per_group)],
+            state_in.at[pl.ds(g * per_group, per_group)],
+            4 + g,
+        )
+        for g in range(GROUPS)
+    ]
+
+    @pl.when(index > 0)
+    def _():
+        pl.semaphore_signal(
+            barrier, inc=1, device_id={"seq": index - 1}, device_id_type=pl.DeviceIdType.MESH
+        )
+
+    @pl.when(index < count - 1)
+    def _():
+        pl.semaphore_wait(barrier, 1)
+        for copy in early:
+            copy.start()
+
+    @pl.when(index == 0)
+    def _():
+        rim_q[...] = jnp.zeros_like(rim_q)
+        rim_k[...] = jnp.zeros_like(rim_k)
+        rim_v[...] = jnp.zeros_like(rim_v)
+        kv_before[...] = jnp.zeros_like(kv_before)
+        state_in[...] = jnp.zeros_like(state_in)
+
+    def arrived(copy):
+        @pl.when(index > 0)
+        def _():
+            copy.wait_recv()
+
+    first = index * rows
+    offsets = [jnp.int32(0)]
+    for d in range(docs - 1):
+        offsets.append(offsets[-1] + doc_ref[d])
+
+    def segments(position):
+        total = jnp.zeros(position.shape, jnp.int32)
+        for offset in offsets:
+            total = total + jnp.where(position >= offset, 1, 0)
+        return total
+
+    square = (rows, rows)
+    row_id = lax.broadcasted_iota(jnp.int32, square, 0)
+    col_id = lax.broadcasted_iota(jnp.int32, square, 1)
+    row_seg = segments(row_id + first)
+    col_seg = segments(col_id + first)
+    before_seg = segments(col_id + (first - rows))
+    visible = (row_id >= col_id) & (row_seg == col_seg)
+    visible_before = row_seg == before_seg
+    strict = (row_id > col_id).astype(F32)
+    carry_mask = row_seg == segments(jnp.zeros(square, jnp.int32) + (first - 1))
+    same = [None] + [
+        jnp.where(row_seg == segments(row_id + (first - s)), 1.0, 0.0) for s in (1, 2, 3)
+    ]
+
+    packed[...] = jnp.zeros_like(packed)
+    packed[:, 0:heads] = log_decay[...]
+    packed[:, heads : 2 * heads] = jax.nn.sigmoid(beta_logit[...])
+    rates = packed[...]
+    part_a = rates.astype(BF)
+    rest = rates - part_a.astype(F32)
+    part_b = rest.astype(BF)
+    part_c = (rest - part_b.astype(F32)).astype(BF)
+    tri = jnp.where(row_id >= col_id, 1.0, 0.0).astype(BF)
+    summed = mm(
+        jnp.concatenate([tri, tri, tri], axis=1), jnp.concatenate([part_a, part_b, part_c], axis=0)
+    )
+    columns = jnp.where(col_id < heads, summed, rates)
+    flipped = columns.T
+    carried = jnp.where(carry_mask & (col_id < heads), jnp.exp(jnp.minimum(columns, 0.0)), 0.0)
+
+    eye = (row_id == col_id).astype(F32)
+
+    def conv(values, spread, rim_ref, taps, at):
+        width = pl.ds(at * LANES, LANES)
+        spread[0:8, width] = rim_ref[rim - 8 : rim, width].astype(F32)
+        spread[8 : 8 + rows, width] = values[:, width].astype(F32)
+        total = spread[8 : 8 + rows, width] * taps[3:4, width].astype(F32)
+        for s in (1, 2, 3):
+            total = total + spread[8 - s : 8 - s + rows, width] * taps[
+                3 - s : 4 - s, width
+            ].astype(F32) * same[s]
+        return total / (1.0 + jnp.exp(-total))
+
+    def unit(x):
+        return x * lax.rsqrt(jnp.sum(x * x, axis=1, keepdims=True) + 1e-06)
+
+    for copy in early[:3]:
+        arrived(copy)
+
+    for g in range(GROUPS):
+        members = range(g * per_group, (g + 1) * per_group)
+        key_heads = range(g * per_group // shared, (g + 1) * per_group // shared)
+        keys, query, scaled_keys, products = {}, {}, {}, {}
+        for p in key_heads:
+            keys[p] = unit(conv(lin_k, spread_k, rim_k, conv_k, p))
+            query[p] = unit(conv(lin_q, spread_q, rim_q, conv_q, p)) * DK ** (-0.5)
+        for p in key_heads:
+            key_high, key_low = halves(keys[p])
+            products[p] = mm(
+                lhs3(jnp.concatenate([query[p], keys[p]], axis=0)),
+                jnp.concatenate([key_high, key_high, key_low], axis=1),
+                transposed=True,
+            )
+            scaled_keys[p] = keys[p].T
+        lower, attend, weigh, right = {}, {}, {}, {}
+        for h in members:
+            p = h // shared
+            gap = columns[:, h : h + 1] - flipped[h : h + 1, :]
+            decay = jnp.exp(jnp.where(visible, gap, NEGATIVE)) * flipped[heads + h : heads + h + 1, :]
+            attend[h] = lhs3(decay * products[p][:rows])
+            lower[h] = decay * strict * products[p][rows:]
+            weigh[h] = lhs3(scaled_keys[p] * decay[rows - 1 : rows, :])
+            right[h] = jnp.concatenate(
+                [conv(lin_v, spread_v, rim_v, conv_v, h), carried[:, h : h + 1] * keys[p]], axis=1
+            )
+        inverse = {}
+        base = 8
+        near = (row_id // base) == (col_id // base)
+        power = {h: jnp.where(near, -lower[h], 0.0).astype(BF) for h in members}
+        whole = {h: power[h].astype(F32) for h in members}
+        power = {h: mm(power[h], power[h]).astype(BF) for h in members}
+        for h in members:
+            both = mm(jnp.concatenate([power[h], whole[h].astype(BF)], axis=0), power[h])
+            whole[h] = whole[h] + power[h].astype(F32) + both[rows:]
+            power[h] = both[:rows].astype(BF)
+        for h in members:
+            whole[h] = whole[h] + power[h].astype(F32) + mm(whole[h].astype(BF), power[h])
+            inverse[h] = eye + whole[h]
+        size = base
+        while size < rows:
+            joint = ((row_id // (2 * size)) == (col_id // (2 * size))) & (
+                (row_id // size) != (col_id // size)
+            )
+            short = {h: inverse[h].astype(BF) for h in members}
+            middle = {
+                h: mm(short[h], jnp.where(joint, lower[h], 0.0).astype(BF)).astype(BF)
+                for h in members
+            }
+            for h in members:
+                inverse[h] = inverse[h] - mm(middle[h], short[h])
+            size *= 2
+        corrector = {h: (inverse[h] - eye).astype(BF) for h in members}
+        solved = {h: right[h] + mm(corrector[h], right[h].astype(BF)) for h in members}
+        residual = {
+            h: right[h] - solved[h] - mm(lhs3(lower[h]), rhs3(solved[h])) for h in members
+        }
+        for h in members:
+            solved[h] = solved[h] + residual[h] + mm(corrector[h], residual[h].astype(BF))
+        stacked = {h: rhs3(solved[h]) for h in members}
+        for h in members:
+            state_out[h] = mm(weigh[h], stacked[h][:, :DV]).astype(BF)
+
+        @pl.when(index < count - 1)
+        def _(g=g):
+            states[g].start()
+
+        for h in members:
+            mixed = mm(attend[h], stacked[h])
+            local_out[h] = mixed[:, :DV]
+            high, low = halves(carried[:, h : h + 1] * query[h // shared] - mixed[:, DV:])
+            reach_out[h] = jnp.concatenate([high, low], axis=1)
+
+    arrived(early[3])
+    score_scale = AD ** (-0.5)
+    allowed = jnp.concatenate([visible_before, visible], axis=1)
+    all_keys = jnp.concatenate([kv_before[:, 0:AD], kv_own[:, 0:AD]], axis=0)
+    all_values = jnp.concatenate([kv_before[:, AD:], kv_own[:, AD:]], axis=0)
+    for a in range(attn_query.shape[1] // AD):
+        width = pl.ds(a * AD, AD)
+        scores = mm(attn_query[:, width], all_keys, transposed=True) * score_scale
+        masked = jnp.where(allowed, scores, NEGATIVE)
+        top = jnp.max(masked, axis=1, keepdims=True)
+        weights = jnp.where(allowed, jnp.exp(masked - top), 0.0)
+        total = jnp.sum(weights, axis=1, keepdims=True)
+        mixture = mm(weights.astype(BF), all_values)
+        gate = attn_gate[:, width].astype(F32)
+        attn_out[:, width] = (mixture / total / (1.0 + jnp.exp(-gate))).astype(BF)
+
+    for g in range(GROUPS):
+        arrived(states[g])
+        for h in range(g * per_group, (g + 1) * per_group):
+            width = pl.ds(h * DV, DV)
+            state = state_in[h]
+            value = local_out[h] + mm(reach_out[h], jnp.concatenate([state, state], axis=0))
+            scale = lax.rsqrt(jnp.mean(value * value, axis=1, keepdims=True) + 1e-06)
+            gate = lin_z[:, width].astype(F32)
+            delta_out[:, width] = (value * scale * (gate / (1.0 + jnp.exp(-gate)))).astype(BF)
+
+    @pl.when(index < count - 1)
+    def _():
+        for copy in early + states:
+            copy.wait_send()
+
+
+def fused(
+    lin_q,
+    lin_k,
+    lin_v,
+    conv_q,
+    conv_k,
+    conv_v,
+    lin_z,
+    beta_logit,
+    log_decay,
+    attn_query,
+    attn_gate,
+    attn_kv,
+    doc_lengths,
+):
+    rows = lin_q.shape[0]
+    heads = lin_v.shape[1] // DV
+    aq_local = attn_query.shape[1] // AD
+    kv_head = lax.axis_index("head") * aq_local // (AQ // KVH)
+    own_pair = lax.dynamic_index_in_dim(attn_kv, kv_head, axis=2, keepdims=False)
+    own_pair = own_pair.reshape(rows, 2 * AD)
+    vmem = pl.BlockSpec(memory_space=pltpu.VMEM)
+    rim = 16
+    copies = 4 + GROUPS
+    return pl.pallas_call(
+        functools.partial(fused_kernel, lax.axis_size("seq")),
+        out_shape=(
+            jax.ShapeDtypeStruct(lin_z.shape, BF),
+            jax.ShapeDtypeStruct(attn_query.shape, BF),
+        ),
+        in_specs=[pl.BlockSpec(memory_space=pltpu.SMEM)] + [vmem] * 12,
+        out_specs=(vmem, vmem),
+        scratch_shapes=[
+            pltpu.VMEM((rim, lin_q.shape[1]), BF),
+            pltpu.VMEM((rim, lin_k.shape[1]), BF),
+            pltpu.VMEM((rim, lin_v.shape[1]), BF),
+            pltpu.VMEM(own_pair.shape, BF),
+            pltpu.VMEM((heads, DK, DV), BF),
+            pltpu.VMEM((heads, DK, DV), BF),
+            pltpu.VMEM((rows + 8, lin_q.shape[1]), F32),
+            pltpu.VMEM((rows + 8, lin_k.shape[1]), F32),
+            pltpu.VMEM((rows + 8, lin_v.shape[1]), F32),
+            pltpu.VMEM((rows, LANES), F32),
+            pltpu.VMEM((heads, rows, DV), F32),
+            pltpu.VMEM((heads, rows, 2 * DK), BF),
+            pltpu.SemaphoreType.DMA((copies,)),
+            pltpu.SemaphoreType.DMA((copies,)),
+        ],
+        compiler_params=pltpu.CompilerParams(
+            collective_id=0, has_side_effects=True, vmem_limit_bytes=48 * 1024 * 1024
+        ),
+    )(
+        doc_lengths,
+        lin_q,
+        lin_k,
+        lin_v,
+        conv_q,
+        conv_k,
+        conv_v,
+        lin_z,
+        beta_logit,
+        log_decay,
+        attn_query,
+        attn_gate,
+        own_pair,
+    )
+
+
 def solution(mesh):
+    near = mesh.shape["seq"] == 4
     return jax.shard_map(
-        shards,
+        fused if near else shards,
         mesh=mesh,
         in_specs=(
             P(("grp", "seq"), "head"),

time: 134 us -> 19.8 us (0.15)
  the two profiles are of different devices: /device:TPU:0 before, /device:TPU:18 now
where the time goes in v1:
time: 19.8 us; the launch traced here: 19.6 us
  Pallas kernels  15 us (76%)
  local copies, waits for them, and re-layouts  3.78 us (19%)
  between operations  0.8 us (4%)
    pallas_call x1, Pallas kernels, fused(): pl.pallas_call(functools.partial(fused_kernel, lax.axis_size('seq')), out...  15 us
    unnamed x31, local copies, waits for them, and re-layouts  3.39 us

profile of v1, /device:TPU:18, one launch (start us, length us, event | category | flops | bytes accessed | tf_op | source)
XLA Modules:
  0.0 19.6 jit_solution(16423230795224161264)
XLA Ops:
  0.6 0.0 copy-start
  0.7 0.0 copy-start.8
  0.7 0.7 %copy-done.11 = f32[128,8]{0,1:T(8,128)S(1)} copy-done((f32[128,8]{0,1:T(8,128)S(1)}, f32[128,8]{0,1:T(8,128)}, u32[]{:S(2)}) %copy-start.11) | copy-done | bytes 4120
  1.4 0.1 copy.18.beta_logit
  1.5 0.0 copy-start.7
  1.5 0.1 copy.19.log_decay
  1.6 0.0 copy-start.3
  1.7 0.0 copy-start.4
  1.7 0.3 %constant_dynamic-slice_fusion = bf16[128,2,1,256]{3,2,1,0:T(2,128)(2,1)S(1)} fusion(bf16[128,2,2,256]{3,2,1,0:T(2,128)(2,1)S(1)} %copy-done, s32[]{:T(128)S(6)} %select_n.10), kind=kLoop, calls=%fused_computation | loop fusion | bytes 262148 | tf_op jit(solution)/shard_map/jit(dynamic_index_in_dim)/dynamic_slice | solution.py:579
  2.0 0.0 copy-start.1
  2.0 0.0 copy-start.2
  2.0 0.2 copy.21
  2.2 0.0 copy-start.5
  2.2 0.0 copy-start.10
  2.2 0.1 copy.20.kv_own
  2.3 0.0 copy-done.6
  2.3 0.3 %copy-done.3 = bf16[128,1024]{1,0:T(8,128)(2,1)S(1)} copy-done((bf16[128,1024]{1,0:T(8,128)(2,1)S(1)}, bf16[128,1024]{1,0:T(8,128)(2,1)}, u32[]{:S(2)}) %copy-start.3) | copy-done | bytes 262168
  2.6 0.1 copy-done.4
  2.7 0.3 %copy-done.1 = bf16[128,1024]{1,0:T(8,128)(2,1)S(1)} copy-done((bf16[128,1024]{1,0:T(8,128)(2,1)S(1)}, bf16[128,1024]{1,0:T(8,128)(2,1)}, u32[]{:S(2)}) %copy-start.1) | copy-done | bytes 262168
  3.0 0.1 copy-done.2
  3.0 0.1 copy-done.5
  3.2 15.0 %shard_map.140 = (bf16[128,1024]{1,0:T(8,128)(2,1)S(1)}, bf16[128,1024]{1,0:T(8,128)(2,1)S(1)}) custom-call(s32[5]{0:T(128)S(1)} %copy-done.10, bf16[128,512]{1,0:T(8,128)(2,1)S(1)} %copy-done.5, bf16[128,512]{1,0:T(8,128)(2,1)S(1)} %copy-done.6, bf16[128,1024]{1,0:T(8,128)(2,1)S(1)} %copy-done.1, bf16[4,512]{1,0:T(4,128)(2,1)S(1)} %copy-done.8, ...), custom_call_target="tpu_custom_call" | custom-call | tf_op jit(solution)/shard_map/pallas_call | solution.py:584
  18.2 0.7 %copy.24 = bf16[128,1024]{1,0:T(8,128)(2,1)} copy(bf16[128,1024]{1,0:T(8,128)(2,1)S(1)} %get-tuple-element.4) | data formatting | bytes 524288
  18.9 0.7 %copy.25 = bf16[128,1024]{1,0:T(8,128)(2,1)} copy(bf16[128,1024]{1,0:T(8,128)(2,1)S(1)} %get-tuple-element.5) | data formatting | bytes 524288
  (10 shorter events, 0.0 us)
Async XLA Ops:
  0.6 1.0 %copy-start = (bf16[128,2,2,256]{3,2,1,0:T(2,128)(2,1)S(1)}, bf16[128,2,2,256]{3,2,1,0:T(2,128)(2,1)}, u32[]{:S(2)}) copy-start(bf16[128,2,2,256]{3,2,1,0:T(2,128)(2,1)} %param.24) | copy-start | bytes 786436
  0.7 0.9 %copy-start.12 = (f32[128,8]{0,1:T(8,128)S(1)}, f32[128,8]{0,1:T(8,128)}, u32[]{:S(2)}) copy-start(f32[128,8]{0,1:T(8,128)} %param.21) | copy-start | bytes 12292
  0.7 1.6 %copy-start.8 = (bf16[4,512]{1,0:T(4,128)(2,1)S(1)}, bf16[4,512]{1,0:T(4,128)(2,1)}, u32[]{:S(2)}) copy-start(bf16[4,512]{1,0:T(4,128)(2,1)} %conv_q.1) | copy-start | bytes 12292
  0.7 1.6 %copy-start.9 = (bf16[4,512]{1,0:T(4,128)(2,1)S(1)}, bf16[4,512]{1,0:T(4,128)(2,1)}, u32[]{:S(2)}) copy-start(bf16[4,512]{1,0:T(4,128)(2,1)} %conv_k.1) | copy-start | bytes 12292
  0.7 0.7 %copy-start.11 = (f32[128,8]{0,1:T(8,128)S(1)}, f32[128,8]{0,1:T(8,128)}, u32[]{:S(2)}) copy-start(f32[128,8]{0,1:T(8,128)} %param.20) | copy-start | bytes 12292
  1.4 0.9 %copy-start.6 = (bf16[128,512]{1,0:T(8,128)(2,1)S(1)}, bf16[128,512]{1,0:T(8,128)(2,1)}, u32[]{:S(2)}) copy-start(bf16[128,512]{1,0:T(8,128)(2,1)} %lin_k.1) | copy-start | bytes 393220
  1.5 0.8 %copy-start.7 = (bf16[4,1024]{1,0:T(4,128)(2,1)S(1)}, bf16[4,1024]{1,0:T(4,128)(2,1)}, u32[]{:S(2)}) copy-start(bf16[4,1024]{1,0:T(4,128)(2,1)} %conv_v.1) | copy-start | bytes 24580
  1.6 1.0 %copy-start.3 = (bf16[128,1024]{1,0:T(8,128)(2,1)S(1)}, bf16[128,1024]{1,0:T(8,128)(2,1)}, u32[]{:S(2)}) copy-start(bf16[128,1024]{1,0:T(8,128)(2,1)} %attn_query.1) | copy-start | bytes 786436
  1.7 1.0 %copy-start.4 = (bf16[128,1024]{1,0:T(8,128)(2,1)S(1)}, bf16[128,1024]{1,0:T(8,128)(2,1)}, u32[]{:S(2)}) copy-start(bf16[128,1024]{1,0:T(8,128)(2,1)} %attn_gate.1) | copy-start | bytes 786436
  2.0 1.0 %copy-start.1 = (bf16[128,1024]{1,0:T(8,128)(2,1)S(1)}, bf16[128,1024]{1,0:T(8,128)(2,1)}, u32[]{:S(2)}) copy-start(bf16[128,1024]{1,0:T(8,128)(2,1)} %lin_v.1) | copy-start | bytes 786436
  2.0 1.1 %copy-start.2 = (bf16[128,1024]{1,0:T(8,128)(2,1)S(1)}, bf16[128,1024]{1,0:T(8,128)(2,1)}, u32[]{:S(2)}) copy-start(bf16[128,1024]{1,0:T(8,128)(2,1)} %lin_z.1) | copy-start | bytes 786436
  2.2 1.0 %copy-start.5 = (bf16[128,512]{1,0:T(8,128)(2,1)S(1)}, bf16[128,512]{1,0:T(8,128)(2,1)}, u32[]{:S(2)}) copy-start(bf16[128,512]{1,0:T(8,128)(2,1)} %lin_q.1) | copy-start | bytes 393220
  2.2 1.0 %copy-start.10 = (s32[5]{0:T(128)S(1)}, s32[5]{0:T(128)}, u32[]{:S(2)}) copy-start(s32[5]{0:T(128)} %doc_ref.1) | copy-start | bytes 64

commit v2 on v1

--- a/solution.py
+++ b/solution.py
@@ -290,19 +290,38 @@
     return high, (x - high.astype(F32)).astype(BF)
 
 
-def lhs3(x):
-    high, low = halves(x)
-    return jnp.concatenate([high, low, high], axis=1)
-
-
-def rhs3(x):
-    high, low = halves(x)
-    return jnp.concatenate([high, high, low], axis=0)
+def block_diagonal(wide):
+    zero = jnp.zeros((wide.shape[0], LANES), wide.dtype)
+    return jnp.concatenate(
+        [
+            jnp.concatenate([wide[:, :LANES], zero], axis=1),
+            jnp.concatenate([zero, wide[:, LANES:]], axis=1),
+        ],
+        axis=0,
+    )
+
+
+def twice(x):
+    return jnp.concatenate([x, x], axis=1)
 
 
 def fused_kernel(
     count,
     doc_ref,
+    kv_own,
+    lin_q_hbm,
+    lin_k_hbm,
+    lin_v_hbm,
+    conv_q_hbm,
+    conv_k_hbm,
+    conv_v_hbm,
+    lin_z_hbm,
+    beta_hbm,
+    decay_hbm,
+    attn_query_hbm,
+    attn_gate_hbm,
+    delta_out,
+    attn_out,
     lin_q,
     lin_k,
     lin_v,
@@ -314,9 +333,6 @@
     log_decay,
     attn_query,
     attn_gate,
-    kv_own,
-    delta_out,
-    attn_out,
     rim_q,
     rim_k,
     rim_v,
@@ -326,19 +342,44 @@
     spread_q,
     spread_k,
     spread_v,
-    packed,
     local_out,
     reach_out,
+    gates,
     send_sem,
     recv_sem,
+    load_sem,
 ):
     rows = lin_q.shape[0]
     heads = lin_v.shape[1] // DV
-    shared = heads // (lin_k.shape[1] // DK)
+    pairs = range(lin_k.shape[1] // DK)
     docs = doc_ref.shape[0]
     rim = rim_q.shape[0]
     index = lax.axis_index("seq")
     barrier = pltpu.get_barrier_semaphore()
+
+    @pl.when(index > 0)
+    def _():
+        pl.semaphore_signal(
+            barrier, inc=1, device_id={"seq": index - 1}, device_id_type=pl.DeviceIdType.MESH
+        )
+
+    loads = {}
+    order = [
+        ("decay", decay_hbm, log_decay),
+        ("beta", beta_hbm, beta_logit),
+        ("taps_k", conv_k_hbm, conv_k),
+        ("k", lin_k_hbm, lin_k),
+        ("taps_v", conv_v_hbm, conv_v),
+        ("v", lin_v_hbm, lin_v),
+        ("taps_q", conv_q_hbm, conv_q),
+        ("q", lin_q_hbm, lin_q),
+        ("query", attn_query_hbm, attn_query),
+        ("gate", attn_gate_hbm, attn_gate),
+        ("z", lin_z_hbm, lin_z),
+    ]
+    for slot, (name, source, target) in enumerate(order):
+        loads[name] = pltpu.make_async_copy(source, target, load_sem.at[slot])
+        loads[name].start()
 
     def transfer(source, target, slot):
         return pltpu.make_async_remote_copy(
@@ -352,26 +393,12 @@
 
     tail = pl.ds(rows - rim, rim)
     early = [
-        transfer(lin_k.at[tail, :], rim_k, 0),
-        transfer(lin_v.at[tail, :], rim_v, 1),
-        transfer(lin_q.at[tail, :], rim_q, 2),
+        transfer(lin_k_hbm.at[tail, :], rim_k, 0),
+        transfer(lin_v_hbm.at[tail, :], rim_v, 1),
+        transfer(lin_q_hbm.at[tail, :], rim_q, 2),
         transfer(kv_own, kv_before, 3),
     ]
-    per_group = heads // GROUPS
-    states = [
-        transfer(
-            state_out.at[pl.ds(g * per_group, per_group)],
-            state_in.at[pl.ds(g * per_group, per_group)],
-            4 + g,
-        )
-        for g in range(GROUPS)
-    ]
-
-    @pl.when(index > 0)
-    def _():
-        pl.semaphore_signal(
-            barrier, inc=1, device_id={"seq": index - 1}, device_id_type=pl.DeviceIdType.MESH
-        )
+    states = transfer(state_out, state_in, 4)
 
     @pl.when(index < count - 1)
     def _():
@@ -387,10 +414,11 @@
         kv_before[...] = jnp.zeros_like(kv_before)
         state_in[...] = jnp.zeros_like(state_in)
 
-    def arrived(copy):
+    def arrived(*copies):
         @pl.when(index > 0)
         def _():
-            copy.wait_recv()
+            for copy in copies:
+                copy.wait_recv()
 
     first = index * rows
     offsets = [jnp.int32(0)]
@@ -411,29 +439,43 @@
     before_seg = segments(col_id + (first - rows))
     visible = (row_id >= col_id) & (row_seg == col_seg)
     visible_before = row_seg == before_seg
-    strict = (row_id > col_id).astype(F32)
-    carry_mask = row_seg == segments(jnp.zeros(square, jnp.int32) + (first - 1))
+    strict = row_id > col_id
     same = [None] + [
         jnp.where(row_seg == segments(row_id + (first - s)), 1.0, 0.0) for s in (1, 2, 3)
     ]
-
-    packed[...] = jnp.zeros_like(packed)
-    packed[:, 0:heads] = log_decay[...]
-    packed[:, heads : 2 * heads] = jax.nn.sigmoid(beta_logit[...])
-    rates = packed[...]
+    short_seg = segments(lax.broadcasted_iota(jnp.int32, (heads, rows), 1) + first)
+    last_seg = segments(jnp.full((heads, rows), rows - 1, jnp.int32) + first)
+    prior_seg = segments(jnp.zeros((heads, rows), jnp.int32) + (first - 1))
+
+    loads["decay"].wait()
+    loads["beta"].wait()
+    rates = log_decay[...]
+    beta = jax.nn.sigmoid(beta_logit[...])
     part_a = rates.astype(BF)
     rest = rates - part_a.astype(F32)
     part_b = rest.astype(BF)
     part_c = (rest - part_b.astype(F32)).astype(BF)
-    tri = jnp.where(row_id >= col_id, 1.0, 0.0).astype(BF)
-    summed = mm(
-        jnp.concatenate([tri, tri, tri], axis=1), jnp.concatenate([part_a, part_b, part_c], axis=0)
-    )
-    columns = jnp.where(col_id < heads, summed, rates)
-    flipped = columns.T
-    carried = jnp.where(carry_mask & (col_id < heads), jnp.exp(jnp.minimum(columns, 0.0)), 0.0)
-
-    eye = (row_id == col_id).astype(F32)
+    upper = jnp.where(row_id <= col_id, 1.0, 0.0).astype(BF)
+    summed = mm(part_a, upper) + mm(part_b, upper) + mm(part_c, upper)
+    carried_row = jnp.where(short_seg == prior_seg, jnp.exp(summed), 0.0)
+    ending = jnp.where(
+        short_seg == last_seg, jnp.exp(summed[:, rows - 1 : rows] - summed), 0.0
+    )
+    columns = jnp.concatenate(
+        [
+            summed,
+            carried_row,
+            beta * ending,
+            jnp.zeros((rows - 3 * heads, rows), F32),
+        ],
+        axis=0,
+    ).T
+    carried = [columns[:, heads + h : heads + h + 1] for h in range(heads)]
+    closing = [columns[:, 2 * heads + h : 2 * heads + h + 1] for h in range(heads)]
+
+    def decays(h):
+        gap = columns[:, h : h + 1] - summed[h : h + 1, :]
+        return jnp.exp(jnp.where(visible, gap, NEGATIVE)) * beta[h : h + 1, :]
 
     def conv(values, spread, rim_ref, taps, at):
         width = pl.ds(at * LANES, LANES)
@@ -449,83 +491,118 @@
     def unit(x):
         return x * lax.rsqrt(jnp.sum(x * x, axis=1, keepdims=True) + 1e-06)
 
-    for copy in early[:3]:
-        arrived(copy)
-
-    for g in range(GROUPS):
-        members = range(g * per_group, (g + 1) * per_group)
-        key_heads = range(g * per_group // shared, (g + 1) * per_group // shared)
-        keys, query, scaled_keys, products = {}, {}, {}, {}
-        for p in key_heads:
-            keys[p] = unit(conv(lin_k, spread_k, rim_k, conv_k, p))
-            query[p] = unit(conv(lin_q, spread_q, rim_q, conv_q, p)) * DK ** (-0.5)
-        for p in key_heads:
-            key_high, key_low = halves(keys[p])
-            products[p] = mm(
-                lhs3(jnp.concatenate([query[p], keys[p]], axis=0)),
-                jnp.concatenate([key_high, key_high, key_low], axis=1),
-                transposed=True,
+    for name in ("taps_k", "k", "taps_v", "v"):
+        loads[name].wait()
+    arrived(*early[:3])
+
+    keys = {p: unit(conv(lin_k, spread_k, rim_k, conv_k, p)) for p in pairs}
+    key_high, key_low, key_right = {}, {}, {}
+    for p in pairs:
+        key_high[p], key_low[p] = halves(keys[p])
+        key_right[p] = jnp.concatenate([key_high[p], key_high[p], key_low[p]], axis=1)
+    lower, decay = {}, {}
+    for p in pairs:
+        product = mm(
+            jnp.concatenate([key_high[p], key_low[p], key_high[p]], axis=1),
+            key_right[p],
+            transposed=True,
+        )
+        product = jnp.where(strict, product, 0.0)
+        for h in (2 * p, 2 * p + 1):
+            decay[h] = decays(h)
+        lower[p] = jnp.concatenate(
+            [decay[2 * p] * product, decay[2 * p + 1] * product], axis=1
+        )
+    base = 8
+    near = twice((row_id // base) == (col_id // base))
+    eye = twice(jnp.where(row_id == col_id, 1.0, 0.0))
+    power = {p: jnp.where(near, -lower[p], 0.0).astype(BF) for p in pairs}
+    whole = {p: power[p].astype(F32) for p in pairs}
+    power = {p: mm(power[p], block_diagonal(power[p])).astype(BF) for p in pairs}
+    for p in pairs:
+        both = mm(
+            jnp.concatenate([power[p], whole[p].astype(BF)], axis=0), block_diagonal(power[p])
+        )
+        whole[p] = whole[p] + power[p].astype(F32) + both[rows:]
+        power[p] = both[:rows].astype(BF)
+    inverse = {
+        p: eye
+        + whole[p]
+        + power[p].astype(F32)
+        + mm(whole[p].astype(BF), block_diagonal(power[p]))
+        for p in pairs
+    }
+    size = base
+    while size < rows:
+        joint = twice(
+            ((row_id // (2 * size)) == (col_id // (2 * size)))
+            & ((row_id // size) != (col_id // size))
+        )
+        short = {p: inverse[p].astype(BF) for p in pairs}
+        middle = {
+            p: mm(short[p], block_diagonal(jnp.where(joint, lower[p], 0.0).astype(BF))).astype(BF)
+            for p in pairs
+        }
+        for p in pairs:
+            inverse[p] = inverse[p] - mm(middle[p], block_diagonal(short[p]))
+        size *= 2
+    corrector, solved, refined, right, split_lower = {}, {}, {}, {}, {}
+    for p in pairs:
+        corrector_pair = (inverse[p] - eye).astype(BF)
+        high, low = halves(lower[p])
+        for half in range(2):
+            h = 2 * p + half
+            lanes = slice(half * LANES, (half + 1) * LANES)
+            corrector[h] = corrector_pair[:, lanes]
+            split_lower[h] = jnp.concatenate([high[:, lanes], low[:, lanes]], axis=1)
+            right[h] = jnp.concatenate(
+                [conv(lin_v, spread_v, rim_v, conv_v, h), carried[h] * keys[p]], axis=1
             )
-            scaled_keys[p] = keys[p].T
-        lower, attend, weigh, right = {}, {}, {}, {}
-        for h in members:
-            p = h // shared
-            gap = columns[:, h : h + 1] - flipped[h : h + 1, :]
-            decay = jnp.exp(jnp.where(visible, gap, NEGATIVE)) * flipped[heads + h : heads + h + 1, :]
-            attend[h] = lhs3(decay * products[p][:rows])
-            lower[h] = decay * strict * products[p][rows:]
-            weigh[h] = lhs3(scaled_keys[p] * decay[rows - 1 : rows, :])
-            right[h] = jnp.concatenate(
-                [conv(lin_v, spread_v, rim_v, conv_v, h), carried[:, h : h + 1] * keys[p]], axis=1
-            )
-        inverse = {}
-        base = 8
-        near = (row_id // base) == (col_id // base)
-        power = {h: jnp.where(near, -lower[h], 0.0).astype(BF) for h in members}
-        whole = {h: power[h].astype(F32) for h in members}
-        power = {h: mm(power[h], power[h]).astype(BF) for h in members}
-        for h in members:
-            both = mm(jnp.concatenate([power[h], whole[h].astype(BF)], axis=0), power[h])
-            whole[h] = whole[h] + power[h].astype(F32) + both[rows:]
-            power[h] = both[:rows].astype(BF)
-        for h in members:
-            whole[h] = whole[h] + power[h].astype(F32) + mm(whole[h].astype(BF), power[h])
-            inverse[h] = eye + whole[h]
-        size = base
-        while size < rows:
-            joint = ((row_id // (2 * size)) == (col_id // (2 * size))) & (
-                (row_id // size) != (col_id // size)
-            )
-            short = {h: inverse[h].astype(BF) for h in members}
-            middle = {
-                h: mm(short[h], jnp.where(joint, lower[h], 0.0).astype(BF)).astype(BF)
-                for h in members
-            }
-            for h in members:
-                inverse[h] = inverse[h] - mm(middle[h], short[h])
-            size *= 2
-        corrector = {h: (inverse[h] - eye).astype(BF) for h in members}
-        solved = {h: right[h] + mm(corrector[h], right[h].astype(BF)) for h in members}
-        residual = {
-            h: right[h] - solved[h] - mm(lhs3(lower[h]), rhs3(solved[h])) for h in members
-        }
-        for h in members:
-            solved[h] = solved[h] + residual[h] + mm(corrector[h], residual[h].astype(BF))
-        stacked = {h: rhs3(solved[h]) for h in members}
-        for h in members:
-            state_out[h] = mm(weigh[h], stacked[h][:, :DV]).astype(BF)
-
-        @pl.when(index < count - 1)
-        def _(g=g):
-            states[g].start()
-
-        for h in members:
-            mixed = mm(attend[h], stacked[h])
+    for h in range(heads):
+        solved[h] = (right[h] + mm(corrector[h], right[h].astype(BF))).astype(BF)
+    for h in range(heads):
+        right[h] = (
+            right[h]
+            - solved[h].astype(F32)
+            - mm(split_lower[h], jnp.concatenate([solved[h], solved[h]], axis=0))
+        )
+    for h in range(heads):
+        refined[h] = (right[h] + mm(corrector[h], right[h].astype(BF))).astype(BF)
+    for p in pairs:
+        parts = [
+            closing[h] * (solved[h][:, :DV].astype(F32) + refined[h][:, :DV].astype(F32))
+            for h in (2 * p, 2 * p + 1)
+        ]
+        wide = jnp.concatenate(parts, axis=1).astype(BF)
+        high, low = halves(keys[p].T)
+        made = mm(
+            jnp.concatenate([high, low], axis=1), jnp.concatenate([wide, wide], axis=0)
+        ).astype(BF)
+        state_out[2 * p] = made[:, :DV]
+        state_out[2 * p + 1] = made[:, DV:]
+
+    @pl.when(index < count - 1)
+    def _():
+        states.start()
+
+    arrived(early[3])
+    for name in ("taps_q", "q", "query", "gate", "z"):
+        loads[name].wait()
+
+    for p in pairs:
+        query = unit(conv(lin_q, spread_q, rim_q, conv_q, p)) * DK ** (-0.5)
+        high, low = halves(query)
+        product = mm(jnp.concatenate([high, low, high], axis=1), key_right[p], transposed=True)
+        for h in (2 * p, 2 * p + 1):
+            high, low = halves(decay[h] * product)
+            mixed = mm(
+                jnp.concatenate([high, low], axis=1),
+                jnp.concatenate([solved[h], solved[h]], axis=0),
+            ) + mm(high, refined[h])
             local_out[h] = mixed[:, :DV]
-            high, low = halves(carried[:, h : h + 1] * query[h // shared] - mixed[:, DV:])
+            high, low = halves(carried[h] * query - mixed[:, DV:])
             reach_out[h] = jnp.concatenate([high, low], axis=1)
 
-    arrived(early[3])
     score_scale = AD ** (-0.5)
     allowed = jnp.concatenate([visible_before, visible], axis=1)
     all_keys = jnp.concatenate([kv_before[:, 0:AD], kv_own[:, 0:AD]], axis=0)
@@ -539,21 +616,21 @@
         total = jnp.sum(weights, axis=1, keepdims=True)
         mixture = mm(weights.astype(BF), all_values)
         gate = attn_gate[:, width].astype(F32)
-        attn_out[:, width] = (mixture / total / (1.0 + jnp.exp(-gate))).astype(BF)
-
-    for g in range(GROUPS):
-        arrived(states[g])
-        for h in range(g * per_group, (g + 1) * per_group):
-            width = pl.ds(h * DV, DV)
-            state = state_in[h]
-            value = local_out[h] + mm(reach_out[h], jnp.concatenate([state, state], axis=0))
-            scale = lax.rsqrt(jnp.mean(value * value, axis=1, keepdims=True) + 1e-06)
-            gate = lin_z[:, width].astype(F32)
-            delta_out[:, width] = (value * scale * (gate / (1.0 + jnp.exp(-gate)))).astype(BF)
+        attn_out[:, width] = (mixture * (1.0 / total) / (1.0 + jnp.exp(-gate))).astype(BF)
+    for h in range(heads):
+        gate = lin_z[:, pl.ds(h * DV, DV)].astype(F32)
+        gates[h] = gate / (1.0 + jnp.exp(-gate))
+
+    arrived(states)
+    for h in range(heads):
+        state = state_in[h]
+        value = local_out[h] + mm(reach_out[h], jnp.concatenate([state, state], axis=0))
+        scale = lax.rsqrt(jnp.mean(value * value, axis=1, keepdims=True) + 1e-06)
+        delta_out[:, pl.ds(h * DV, DV)] = (value * scale * gates[h]).astype(BF)
 
     @pl.when(index < count - 1)
     def _():
-        for copy in early + states:
+        for copy in early + [states]:
             copy.wait_send()
 
 
@@ -578,18 +655,32 @@
     kv_head = lax.axis_index("head") * aq_local // (AQ // KVH)
     own_pair = lax.dynamic_index_in_dim(attn_kv, kv_head, axis=2, keepdims=False)
     own_pair = own_pair.reshape(rows, 2 * AD)
+    streamed = (
+        lin_q,
+        lin_k,
+        lin_v,
+        conv_q,
+        conv_k,
+        conv_v,
+        lin_z,
+        beta_logit.T,
+        log_decay.T,
+        attn_query,
+        attn_gate,
+    )
     vmem = pl.BlockSpec(memory_space=pltpu.VMEM)
     rim = 16
-    copies = 4 + GROUPS
     return pl.pallas_call(
         functools.partial(fused_kernel, lax.axis_size("seq")),
         out_shape=(
             jax.ShapeDtypeStruct(lin_z.shape, BF),
             jax.ShapeDtypeStruct(attn_query.shape, BF),
         ),
-        in_specs=[pl.BlockSpec(memory_space=pltpu.SMEM)] + [vmem] * 12,
+        in_specs=[pl.BlockSpec(memory_space=pltpu.SMEM), vmem]
+        + [pl.BlockSpec(memory_space=pltpu.HBM)] * len(streamed),
         out_specs=(vmem, vmem),
-        scratch_shapes=[
+        scratch_shapes=[pltpu.VMEM(x.shape, x.dtype) for x in streamed]
+        + [
             pltpu.VMEM((rim, lin_q.shape[1]), BF),
             pltpu.VMEM((rim, lin_k.shape[1]), BF),
             pltpu.VMEM((rim, lin_v.shape[1]), BF),
@@ -599,30 +690,17 @@
             pltpu.VMEM((rows + 8, lin_q.shape[1]), F32),
             pltpu.VMEM((rows + 8, lin_k.shape[1]), F32),
             pltpu.VMEM((rows + 8, lin_v.shape[1]), F32),
-            pltpu.VMEM((rows, LANES), F32),
             pltpu.VMEM((heads, rows, DV), F32),
             pltpu.VMEM((heads, rows, 2 * DK), BF),
-            pltpu.SemaphoreType.DMA((copies,)),
-            pltpu.SemaphoreType.DMA((copies,)),
+            pltpu.VMEM((heads, rows, DV), F32),
+            pltpu.SemaphoreType.DMA((5,)),
+            pltpu.SemaphoreType.DMA((5,)),
+            pltpu.SemaphoreType.DMA((len(streamed),)),
         ],
         compiler_params=pltpu.CompilerParams(
             collective_id=0, has_side_effects=True, vmem_limit_bytes=48 * 1024 * 1024
         ),
-    )(
-        doc_lengths,
-        lin_q,
-        lin_k,
-        lin_v,
-        conv_q,
-        conv_k,
-        conv_v,
-        lin_z,
-        beta_logit,
-        log_decay,
-        attn_query,
-        attn_gate,
-        own_pair,
-    )
+    )(doc_lengths, own_pair, *streamed)
 
 
 def solution(mesh):

time: 19.8 us -> 19.7 us (level)
  Pallas kernels: 15 us -> 14.1 us
  local copies, waits for them, and re-layouts: 3.78 us -> 4.6 us
    pallas_call x1, Pallas kernels: 15 us -> 14.1 us  [fused(): pl.pallas_call(functools.partial(fused_kernel, lax.axis_size('seq')), out...]
    unnamed x31 -> x29, local copies, waits for them, and re-layouts: 3.39 us -> 4.21 us
where the time goes in v2:
time: 19.7 us; the launch traced here: 19.5 us
  Pallas kernels  14.1 us (72%)
  local copies, waits for them, and re-layouts  4.6 us (23%)
  between operations  0.79 us (4%)
    pallas_call x1, Pallas kernels, fused(): pl.pallas_call(functools.partial(fused_kernel, lax.axis_size('seq')), out...  14.1 us
    unnamed x29, local copies, waits for them, and re-layouts  4.21 us

profile of v2, /device:TPU:18, one launch (start us, length us, event | category | flops | bytes accessed | tf_op | source)
XLA Modules:
  0.0 19.5 jit_solution(6382028907390852617)
XLA Ops:
  0.6 0.0 copy-start
  0.7 0.0 copy-start.9
  0.7 0.0 copy-start.10
  0.7 0.0 copy-start.11
  0.7 0.0 copy-start.7
  0.7 0.0 copy-start.8
  0.7 0.9 %copy-done = bf16[128,2,2,256]{3,2,1,0:T(2,128)(2,1)S(1)} copy-done((bf16[128,2,2,256]{3,2,1,0:T(2,128)(2,1)S(1)}, bf16[128,2,2,256]{3,2,1,0:T(2,128)(2,1)}, u32[]{:S(2)}) %copy-start) | copy-done | bytes 262168
  1.6 0.3 %constant_dynamic-slice_fusion = bf16[128,2,1,256]{3,2,1,0:T(2,128)(2,1)S(1)} fusion(bf16[128,2,2,256]{3,2,1,0:T(2,128)(2,1)S(1)} %copy-done, s32[]{:T(128)S(6)} %select_n.10), kind=kLoop, calls=%fused_computation | loop fusion | bytes 262148 | tf_op jit(solution)/shard_map/jit(dynamic_index_in_dim)/dynamic_slice | solution.py:656
  1.9 0.0 copy-start.1
  1.9 0.0 copy-start.2
  1.9 0.2 copy.17
  2.1 0.0 copy-start.5
  2.1 0.0 copy-start.12
  2.1 0.1 copy.16.kv_own
  2.2 0.0 copy-done.9
  2.3 0.3 %copy-done.3 = bf16[128,1024]{1,0:T(8,128)(2,1)S(1)} copy-done((bf16[128,1024]{1,0:T(8,128)(2,1)S(1)}, bf16[128,1024]{1,0:T(8,128)(2,1)}, u32[]{:S(2)}) %copy-start.3) | copy-done | bytes 262168
  2.5 0.1 copy-done.4
  2.6 0.2 %copy-done.1 = bf16[128,1024]{1,0:T(8,128)(2,1)S(1)} copy-done((bf16[128,1024]{1,0:T(8,128)(2,1)S(1)}, bf16[128,1024]{1,0:T(8,128)(2,1)}, u32[]{:S(2)}) %copy-start.1) | copy-done | bytes 262168
  2.9 0.1 copy-done.2
  2.9 0.1 copy-done.5
  3.1 0.9 %copy-done.6 = bf16[128,512]{1,0:T(8,128)(2,1)S(1)} copy-done((bf16[128,512]{1,0:T(8,128)(2,1)S(1)}, bf16[128,512]{1,0:T(8,128)(2,1)}, u32[]{:S(2)}) %copy-start.6) | copy-done | bytes 131096
  4.0 14.1 %shard_map.140 = (bf16[128,1024]{1,0:T(8,128)(2,1)S(1)}, bf16[128,1024]{1,0:T(8,128)(2,1)S(1)}) custom-call(s32[5]{0:T(128)S(1)} %copy-done.12, bf16[128,512]{1,0:T(8,128)(2,1)S(1)} %copy.16.kv_own, bf16[128,512]{1,0:T(8,128)(2,1)S(1)} %copy-done.5, bf16[128,512]{1,0:T(8,128)(2,1)S(1)} %copy-done.6, bf16[128,1024]{1,0:T(8,128)(2,1)S(1)} %copy-done.1, ...), custom_call_target="tpu_custom_call" | custom-call | tf_op jit(solution)/shard_map/pallas_call | solution.py:673
  18.1 0.7 %copy.20 = bf16[128,1024]{1,0:T(8,128)(2,1)} copy(bf16[128,1024]{1,0:T(8,128)(2,1)S(1)} %get-tuple-element.4) | data formatting | bytes 524288
  18.8 0.7 %copy.21 = bf16[128,1024]{1,0:T(8,128)(2,1)} copy(bf16[128,1024]{1,0:T(8,128)(2,1)S(1)} %get-tuple-element.5) | data formatting | bytes 524288
  (8 shorter events, 0.0 us)
Async XLA Ops:
  0.6 1.0 %copy-start = (bf16[128,2,2,256]{3,2,1,0:T(2,128)(2,1)S(1)}, bf16[128,2,2,256]{3,2,1,0:T(2,128)(2,1)}, u32[]{:S(2)}) copy-start(bf16[128,2,2,256]{3,2,1,0:T(2,128)(2,1)} %param.24) | copy-start | bytes 786436
  0.7 1.6 %copy-start.9 = (bf16[4,512]{1,0:T(4,128)(2,1)S(1)}, bf16[4,512]{1,0:T(4,128)(2,1)}, u32[]{:S(2)}) copy-start(bf16[4,512]{1,0:T(4,128)(2,1)} %conv_k_hbm.1) | copy-start | bytes 12292
  0.7 1.6 %copy-start.10 = (f32[128,8]{0,1:T(8,128)S(1)}, f32[128,8]{0,1:T(8,128)}, u32[]{:S(2)}) copy-start(f32[128,8]{0,1:T(8,128)} %param.20) | copy-start | bytes 12292
  0.7 1.6 %copy-start.11 = (f32[128,8]{0,1:T(8,128)S(1)}, f32[128,8]{0,1:T(8,128)}, u32[]{:S(2)}) copy-start(f32[128,8]{0,1:T(8,128)} %param.21) | copy-start | bytes 12292
  0.7 1.6 %copy-start.7 = (bf16[4,1024]{1,0:T(4,128)(2,1)S(1)}, bf16[4,1024]{1,0:T(4,128)(2,1)}, u32[]{:S(2)}) copy-start(bf16[4,1024]{1,0:T(4,128)(2,1)} %conv_v_hbm.1) | copy-start | bytes 24580
  0.7 1.6 %copy-start.8 = (bf16[4,512]{1,0:T(4,128)(2,1)S(1)}, bf16[4,512]{1,0:T(4,128)(2,1)}, u32[]{:S(2)}) copy-start(bf16[4,512]{1,0:T(4,128)(2,1)} %conv_q_hbm.1) | copy-start | bytes 12292
  1.6 0.9 %copy-start.3 = (bf16[128,1024]{1,0:T(8,128)(2,1)S(1)}, bf16[128,1024]{1,0:T(8,128)(2,1)}, u32[]{:S(2)}) copy-start(bf16[128,1024]{1,0:T(8,128)(2,1)} %attn_query_hbm.1) | copy-start | bytes 786436
  1.6 1.0 %copy-start.4 = (bf16[128,1024]{1,0:T(8,128)(2,1)S(1)}, bf16[128,1024]{1,0:T(8,128)(2,1)}, u32[]{:S(2)}) copy-start(bf16[128,1024]{1,0:T(8,128)(2,1)} %attn_gate_hbm.1) | copy-start | bytes 786436
  1.9 1.0 %copy-start.1 = (bf16[128,1024]{1,0:T(8,128)(2,1)S(1)}, bf16[128,1024]{1,0:T(8,128)(2,1)}, u32[]{:S(2)}) copy-start(bf16[128,1024]{1,0:T(8,128)(2,1)} %lin_v_hbm.1) | copy-start | bytes 786436
  1.9 1.1 %copy-start.2 = (bf16[128,1024]{1,0:T(8,128)(2,1)S(1)}, bf16[128,1024]{1,0:T(8,128)(2,1)}, u32[]{:S(2)}) copy-start(bf16[128,1024]{1,0:T(8,128)(2,1)} %lin_z_hbm.1) | copy-start | bytes 786436
  2.1 1.0 %copy-start.5 = (bf16[128,512]{1,0:T(8,128)(2,1)S(1)}, bf16[128,512]{1,0:T(8,128)(2,1)}, u32[]{:S(2)}) copy-start(bf16[128,512]{1,0:T(8,128)(2,1)} %lin_q_hbm.1) | copy-start | bytes 393220
  2.1 1.0 %copy-start.12 = (s32[5]{0:T(128)S(1)}, s32[5]{0:T(128)}, u32[]{:S(2)}) copy-start(s32[5]{0:T(128)} %doc_ref.1) | copy-start | bytes 64
  3.1 0.9 %copy-start.6 = (bf16[128,512]{1,0:T(8,128)(2,1)S(1)}, bf16[128,512]{1,0:T(8,128)(2,1)}, u32[]{:S(2)}) copy-start(bf16[128,512]{1,0:T(8,128)(2,1)} %lin_k_hbm.1) | copy-start | bytes 393220

commit v3 on v2

--- a/solution.py
+++ b/solution.py
@@ -367,6 +367,7 @@
     order = [
         ("decay", decay_hbm, log_decay),
         ("beta", beta_hbm, beta_logit),
+        ("z", lin_z_hbm, lin_z),
         ("taps_k", conv_k_hbm, conv_k),
         ("k", lin_k_hbm, lin_k),
         ("taps_v", conv_v_hbm, conv_v),
@@ -375,7 +376,6 @@
         ("q", lin_q_hbm, lin_q),
         ("query", attn_query_hbm, attn_query),
         ("gate", attn_gate_hbm, attn_gate),
-        ("z", lin_z_hbm, lin_z),
     ]
     for slot, (name, source, target) in enumerate(order):
         loads[name] = pltpu.make_async_copy(source, target, load_sem.at[slot])
@@ -398,7 +398,11 @@
         transfer(lin_q_hbm.at[tail, :], rim_q, 2),
         transfer(kv_own, kv_before, 3),
     ]
-    states = transfer(state_out, state_in, 4)
+    per_group = len(pairs) // GROUPS
+    states = []
+    for g in range(GROUPS):
+        part = pl.ds(g * 2 * per_group, 2 * per_group)
+        states.append(transfer(state_out.at[part], state_in.at[part], 4 + g))
 
     @pl.when(index < count - 1)
     def _():
@@ -491,102 +495,113 @@
     def unit(x):
         return x * lax.rsqrt(jnp.sum(x * x, axis=1, keepdims=True) + 1e-06)
 
+    loads["z"].wait()
+    for h in range(heads):
+        gate = lin_z[:, pl.ds(h * DV, DV)].astype(F32)
+        gates[h] = gate / (1.0 + jnp.exp(-gate))
     for name in ("taps_k", "k", "taps_v", "v"):
         loads[name].wait()
-    arrived(*early[:3])
-
-    keys = {p: unit(conv(lin_k, spread_k, rim_k, conv_k, p)) for p in pairs}
-    key_high, key_low, key_right = {}, {}, {}
-    for p in pairs:
-        key_high[p], key_low[p] = halves(keys[p])
-        key_right[p] = jnp.concatenate([key_high[p], key_high[p], key_low[p]], axis=1)
-    lower, decay = {}, {}
-    for p in pairs:
-        product = mm(
-            jnp.concatenate([key_high[p], key_low[p], key_high[p]], axis=1),
-            key_right[p],
-            transposed=True,
-        )
-        product = jnp.where(strict, product, 0.0)
-        for h in (2 * p, 2 * p + 1):
-            decay[h] = decays(h)
-        lower[p] = jnp.concatenate(
-            [decay[2 * p] * product, decay[2 * p + 1] * product], axis=1
-        )
-    base = 8
-    near = twice((row_id // base) == (col_id // base))
-    eye = twice(jnp.where(row_id == col_id, 1.0, 0.0))
-    power = {p: jnp.where(near, -lower[p], 0.0).astype(BF) for p in pairs}
-    whole = {p: power[p].astype(F32) for p in pairs}
-    power = {p: mm(power[p], block_diagonal(power[p])).astype(BF) for p in pairs}
-    for p in pairs:
-        both = mm(
-            jnp.concatenate([power[p], whole[p].astype(BF)], axis=0), block_diagonal(power[p])
-        )
-        whole[p] = whole[p] + power[p].astype(F32) + both[rows:]
-        power[p] = both[:rows].astype(BF)
-    inverse = {
-        p: eye
-        + whole[p]
-        + power[p].astype(F32)
-        + mm(whole[p].astype(BF), block_diagonal(power[p]))
-        for p in pairs
-    }
-    size = base
-    while size < rows:
-        joint = twice(
-            ((row_id // (2 * size)) == (col_id // (2 * size)))
-            & ((row_id // size) != (col_id // size))
-        )
-        short = {p: inverse[p].astype(BF) for p in pairs}
-        middle = {
-            p: mm(short[p], block_diagonal(jnp.where(joint, lower[p], 0.0).astype(BF))).astype(BF)
+    arrived(*early[:2])
+
+    def make_states(pairs):
+        for p in pairs:
+            keys[p] = unit(conv(lin_k, spread_k, rim_k, conv_k, p))
+        for p in pairs:
+            key_high[p], key_low[p] = halves(keys[p])
+            key_right[p] = jnp.concatenate([key_high[p], key_high[p], key_low[p]], axis=1)
+        lower = {}
+        for p in pairs:
+            product = mm(
+                jnp.concatenate([key_high[p], key_low[p], key_high[p]], axis=1),
+                key_right[p],
+                transposed=True,
+            )
+            product = jnp.where(strict, product, 0.0)
+            for h in (2 * p, 2 * p + 1):
+                decay[h] = decays(h)
+            lower[p] = jnp.concatenate(
+                [decay[2 * p] * product, decay[2 * p + 1] * product], axis=1
+            )
+        base = 8
+        near = twice((row_id // base) == (col_id // base))
+        eye = twice(jnp.where(row_id == col_id, 1.0, 0.0))
+        power = {p: jnp.where(near, -lower[p], 0.0).astype(BF) for p in pairs}
+        whole = {p: power[p].astype(F32) for p in pairs}
+        power = {p: mm(power[p], block_diagonal(power[p])).astype(BF) for p in pairs}
+        for p in pairs:
+            both = mm(
+                jnp.concatenate([power[p], whole[p].astype(BF)], axis=0), block_diagonal(power[p])
+            )
+            whole[p] = whole[p] + power[p].astype(F32) + both[rows:]
+            power[p] = both[:rows].astype(BF)
+        inverse = {
+            p: eye
+            + whole[p]
+            + power[p].astype(F32)
+            + mm(whole[p].astype(BF), block_diagonal(power[p]))
             for p in pairs
         }
+        size = base
+        while size < rows:
+            joint = twice(
+                ((row_id // (2 * size)) == (col_id // (2 * size)))
+                & ((row_id // size) != (col_id // size))
+            )
+            short = {p: inverse[p].astype(BF) for p in pairs}
+            middle = {
+                p: mm(short[p], block_diagonal(jnp.where(joint, lower[p], 0.0).astype(BF))).astype(BF)
+                for p in pairs
+            }
+            for p in pairs:
+                inverse[p] = inverse[p] - mm(middle[p], block_diagonal(short[p]))
+            size *= 2
+        corrector, right, split_lower = {}, {}, {}
+        members = [2 * p + half for p in pairs for half in range(2)]
         for p in pairs:
-            inverse[p] = inverse[p] - mm(middle[p], block_diagonal(short[p]))
-        size *= 2
-    corrector, solved, refined, right, split_lower = {}, {}, {}, {}, {}
-    for p in pairs:
-        corrector_pair = (inverse[p] - eye).astype(BF)
-        high, low = halves(lower[p])
-        for half in range(2):
-            h = 2 * p + half
-            lanes = slice(half * LANES, (half + 1) * LANES)
-            corrector[h] = corrector_pair[:, lanes]
-            split_lower[h] = jnp.concatenate([high[:, lanes], low[:, lanes]], axis=1)
-            right[h] = jnp.concatenate(
-                [conv(lin_v, spread_v, rim_v, conv_v, h), carried[h] * keys[p]], axis=1
+            corrector_pair = (inverse[p] - eye).astype(BF)
+            high, low = halves(lower[p])
+            for half in range(2):
+                h = 2 * p + half
+                lanes = slice(half * LANES, (half + 1) * LANES)
+                corrector[h] = corrector_pair[:, lanes]
+                split_lower[h] = jnp.concatenate([high[:, lanes], low[:, lanes]], axis=1)
+                right[h] = jnp.concatenate(
+                    [conv(lin_v, spread_v, rim_v, conv_v, h), carried[h] * keys[p]], axis=1
+                )
+        for h in members:
+            solved[h] = (right[h] + mm(corrector[h], right[h].astype(BF))).astype(BF)
+        for h in members:
+            right[h] = (
+                right[h]
+                - solved[h].astype(F32)
+                - mm(split_lower[h], jnp.concatenate([solved[h], solved[h]], axis=0))
             )
-    for h in range(heads):
-        solved[h] = (right[h] + mm(corrector[h], right[h].astype(BF))).astype(BF)
-    for h in range(heads):
-        right[h] = (
-            right[h]
-            - solved[h].astype(F32)
-            - mm(split_lower[h], jnp.concatenate([solved[h], solved[h]], axis=0))
-        )
-    for h in range(heads):
-        refined[h] = (right[h] + mm(corrector[h], right[h].astype(BF))).astype(BF)
-    for p in pairs:
-        parts = [
-            closing[h] * (solved[h][:, :DV].astype(F32) + refined[h][:, :DV].astype(F32))
-            for h in (2 * p, 2 * p + 1)
-        ]
-        wide = jnp.concatenate(parts, axis=1).astype(BF)
-        high, low = halves(keys[p].T)
-        made = mm(
-            jnp.concatenate([high, low], axis=1), jnp.concatenate([wide, wide], axis=0)
-        ).astype(BF)
-        state_out[2 * p] = made[:, :DV]
-        state_out[2 * p + 1] = made[:, DV:]
-
-    @pl.when(index < count - 1)
-    def _():
-        states.start()
-
-    arrived(early[3])
-    for name in ("taps_q", "q", "query", "gate", "z"):
+        for h in members:
+            refined[h] = (right[h] + mm(corrector[h], right[h].astype(BF))).astype(BF)
+        for p in pairs:
+            parts = [
+                closing[h] * (solved[h][:, :DV].astype(F32) + refined[h][:, :DV].astype(F32))
+                for h in (2 * p, 2 * p + 1)
+            ]
+            wide = jnp.concatenate(parts, axis=1).astype(BF)
+            high, low = halves(keys[p].T)
+            made = mm(
+                jnp.concatenate([high, low], axis=1), jnp.concatenate([wide, wide], axis=0)
+            ).astype(BF)
+            state_out[2 * p] = made[:, :DV]
+            state_out[2 * p + 1] = made[:, DV:]
+
+    keys, key_high, key_low, key_right, decay = {}, {}, {}, {}, {}
+    solved, refined = {}, {}
+    for g in range(GROUPS):
+        make_states(pairs[g * per_group : (g + 1) * per_group])
+
+        @pl.when(index < count - 1)
+        def _(g=g):
+            states[g].start()
+
+    arrived(early[2], early[3])
+    for name in ("taps_q", "q", "query", "gate"):
         loads[name].wait()
 
     for p in pairs:
@@ -617,12 +632,10 @@
         mixture = mm(weights.astype(BF), all_values)
         gate = attn_gate[:, width].astype(F32)
         attn_out[:, width] = (mixture * (1.0 / total) / (1.0 + jnp.exp(-gate))).astype(BF)
+
     for h in range(heads):
-        gate = lin_z[:, pl.ds(h * DV, DV)].astype(F32)
-        gates[h] = gate / (1.0 + jnp.exp(-gate))
-
-    arrived(states)
-    for h in range(heads):
+        if h % (2 * per_group) == 0:
+            arrived(states[h // (2 * per_group)])
         state = state_in[h]
         value = local_out[h] + mm(reach_out[h], jnp.concatenate([state, state], axis=0))
         scale = lax.rsqrt(jnp.mean(value * value, axis=1, keepdims=True) + 1e-06)
@@ -630,7 +643,7 @@
 
     @pl.when(index < count - 1)
     def _():
-        for copy in early + [states]:
+        for copy in early + states:
             copy.wait_send()
 
 
@@ -693,12 +706,12 @@
             pltpu.VMEM((heads, rows, DV), F32),
             pltpu.VMEM((heads, rows, 2 * DK), BF),
             pltpu.VMEM((heads, rows, DV), F32),
-            pltpu.SemaphoreType.DMA((5,)),
-            pltpu.SemaphoreType.DMA((5,)),
+            pltpu.SemaphoreType.DMA((4 + GROUPS,)),
+            pltpu.SemaphoreType.DMA((4 + GROUPS,)),
             pltpu.SemaphoreType.DMA((len(streamed),)),
         ],
         compiler_params=pltpu.CompilerParams(
-            collective_id=0, has_side_effects=True, vmem_limit_bytes=48 * 1024 * 1024
+            collective_id=0, has_side_effects=True, vmem_limit_bytes=56 * 1024 * 1024
         ),
     )(doc_lengths, own_pair, *streamed)
 

time: 19.7 us -> 21.3 us (1.081)
  Pallas kernels: 14.1 us -> 15.9 us
    pallas_call x1, Pallas kernels: 14.1 us -> 15.9 us  [fused(): pl.pallas_call(functools.partial(fused_kernel, lax.axis_size('seq')), out...]
    unnamed x29 -> x7, local copies, waits for them, and re-layouts: 4.21 us -> 3.53 us
    reshape x1, local copies, waits for them, and re-layouts: 0.11 us -> 0.77 us  [fused(): own_pair = own_pair.reshape(rows, 2 * AD)]
where the time goes in v3:
time: 21.3 us; the launch traced here: 21.1 us
  Pallas kernels  15.9 us (75%)
  local copies, waits for them, and re-layouts  4.58 us (22%)
  between operations  0.68 us (3%)
    pallas_call x1, Pallas kernels, fused(): pl.pallas_call(functools.partial(fused_kernel, lax.axis_size('seq')), out...  15.9 us
    unnamed x7, local copies, waits for them, and re-layouts  3.53 us
    reshape x1, local copies, waits for them, and re-layouts, fused(): own_pair = own_pair.reshape(rows, 2 * AD)  0.77 us

profile of v3, /device:TPU:18, one launch (start us, length us, event | category | flops | bytes accessed | tf_op | source)
XLA Modules:
  0.0 21.1 jit_solution(2288180224548418490)
XLA Ops:
  0.6 0.0 copy-start
  0.7 0.9 %copy-done = bf16[128,2,2,256]{3,2,1,0:T(2,128)(2,1)S(1)} copy-done((bf16[128,2,2,256]{3,2,1,0:T(2,128)(2,1)S(1)}, bf16[128,2,2,256]{3,2,1,0:T(2,128)(2,1)}, u32[]{:S(2)}) %copy-start) | copy-done | bytes 262168
  1.6 0.3 %constant_dynamic-slice_fusion = bf16[128,2,1,256]{3,2,1,0:T(2,128)(2,1)S(1)} fusion(bf16[128,2,2,256]{3,2,1,0:T(2,128)(2,1)S(1)} %copy-done, s32[]{:T(128)S(6)} %select_n.10), kind=kLoop, calls=%fused_computation | loop fusion | bytes 262148 | tf_op jit(solution)/shard_map/jit(dynamic_index_in_dim)/dynamic_slice | solution.py:669
  1.9 0.2 copy.17
  2.0 0.8 %copy.16.kv_own = bf16[128,512]{1,0:T(8,128)(2,1)} copy(bf16[128,512]{0,1:T(8,128)(2,1)S(1)} %bitcast.3) | data formatting | bytes 262144 | tf_op jit(solution)/shard_map/reshape | solution.py:670
  2.8 15.9 %shard_map.140 = (bf16[128,1024]{1,0:T(8,128)(2,1)}, bf16[128,1024]{1,0:T(8,128)(2,1)}) custom-call(s32[5]{0:T(128)} %doc_ref.1, bf16[128,512]{1,0:T(8,128)(2,1)} %copy.16.kv_own, bf16[128,512]{1,0:T(8,128)(2,1)} %lin_q_hbm.1, bf16[128,512]{1,0:T(8,128)(2,1)} %lin_k_hbm.1, bf16[128,1024]{1,0:T(8,128)(2,1)} %lin_v_hbm.1, bf16[4,512]{1,0:T(4,128)(2,1)} %conv_q_hbm.1, ...), custom_call_target="tpu_custom_call" | custom-call | tf_op jit(solution)/shard_map/pallas_call | solution.py:686
  18.7 0.0 copy-start.1
  18.7 1.7 %copy.20 = bf16[128,1024]{1,0:T(8,128)(2,1)} copy(bf16[128,1024]{1,0:T(8,128)(2,1)} %get-tuple-element.4) | data formatting | bytes 524288
  20.4 0.0 copy-done.1
  20.4 0.7 %copy.21 = bf16[128,1024]{1,0:T(8,128)(2,1)} copy(bf16[128,1024]{1,0:T(8,128)(2,1)S(1)} %copy-done.1) | data formatting | bytes 524288
Async XLA Ops:
  0.6 1.0 %copy-start = (bf16[128,2,2,256]{3,2,1,0:T(2,128)(2,1)S(1)}, bf16[128,2,2,256]{3,2,1,0:T(2,128)(2,1)}, u32[]{:S(2)}) copy-start(bf16[128,2,2,256]{3,2,1,0:T(2,128)(2,1)} %param.24) | copy-start | bytes 786436
  18.7 1.7 %copy-start.1 = (bf16[128,1024]{1,0:T(8,128)(2,1)S(1)}, bf16[128,1024]{1,0:T(8,128)(2,1)}, u32[]{:S(2)}) copy-start(bf16[128,1024]{1,0:T(8,128)(2,1)} %get-tuple-element.5) | copy-start | bytes 786436

commit v4 on v2

--- a/solution.py
+++ b/solution.py
@@ -309,19 +309,6 @@
     count,
     doc_ref,
     kv_own,
-    lin_q_hbm,
-    lin_k_hbm,
-    lin_v_hbm,
-    conv_q_hbm,
-    conv_k_hbm,
-    conv_v_hbm,
-    lin_z_hbm,
-    beta_hbm,
-    decay_hbm,
-    attn_query_hbm,
-    attn_gate_hbm,
-    delta_out,
-    attn_out,
     lin_q,
     lin_k,
     lin_v,
@@ -333,6 +320,8 @@
     log_decay,
     attn_query,
     attn_gate,
+    delta_out,
+    attn_out,
     rim_q,
     rim_k,
     rim_v,
@@ -347,7 +336,6 @@
     gates,
     send_sem,
     recv_sem,
-    load_sem,
 ):
     rows = lin_q.shape[0]
     heads = lin_v.shape[1] // DV
@@ -363,24 +351,6 @@
             barrier, inc=1, device_id={"seq": index - 1}, device_id_type=pl.DeviceIdType.MESH
         )
 
-    loads = {}
-    order = [
-        ("decay", decay_hbm, log_decay),
-        ("beta", beta_hbm, beta_logit),
-        ("taps_k", conv_k_hbm, conv_k),
-        ("k", lin_k_hbm, lin_k),
-        ("taps_v", conv_v_hbm, conv_v),
-        ("v", lin_v_hbm, lin_v),
-        ("taps_q", conv_q_hbm, conv_q),
-        ("q", lin_q_hbm, lin_q),
-        ("query", attn_query_hbm, attn_query),
-        ("gate", attn_gate_hbm, attn_gate),
-        ("z", lin_z_hbm, lin_z),
-    ]
-    for slot, (name, source, target) in enumerate(order):
-        loads[name] = pltpu.make_async_copy(source, target, load_sem.at[slot])
-        loads[name].start()
-
     def transfer(source, target, slot):
         return pltpu.make_async_remote_copy(
             src_ref=source,
@@ -393,12 +363,16 @@
 
     tail = pl.ds(rows - rim, rim)
     early = [
-        transfer(lin_k_hbm.at[tail, :], rim_k, 0),
-        transfer(lin_v_hbm.at[tail, :], rim_v, 1),
-        transfer(lin_q_hbm.at[tail, :], rim_q, 2),
+        transfer(lin_k.at[tail, :], rim_k, 0),
+        transfer(lin_v.at[tail, :], rim_v, 1),
+        transfer(lin_q.at[tail, :], rim_q, 2),
         transfer(kv_own, kv_before, 3),
     ]
-    states = transfer(state_out, state_in, 4)
+    per_group = heads // GROUPS
+    states = []
+    for g in range(GROUPS):
+        part = pl.ds(g * per_group, per_group)
+        states.append(transfer(state_out.at[part], state_in.at[part], 4 + g))
 
     @pl.when(index < count - 1)
     def _():
@@ -447,8 +421,6 @@
     last_seg = segments(jnp.full((heads, rows), rows - 1, jnp.int32) + first)
     prior_seg = segments(jnp.zeros((heads, rows), jnp.int32) + (first - 1))
 
-    loads["decay"].wait()
-    loads["beta"].wait()
     rates = log_decay[...]
     beta = jax.nn.sigmoid(beta_logit[...])
     part_a = rates.astype(BF)
@@ -491,9 +463,7 @@
     def unit(x):
         return x * lax.rsqrt(jnp.sum(x * x, axis=1, keepdims=True) + 1e-06)
 
-    for name in ("taps_k", "k", "taps_v", "v"):
-        loads[name].wait()
-    arrived(*early[:3])
+    arrived(*early[:2])
 
     keys = {p: unit(conv(lin_k, spread_k, rim_k, conv_k, p)) for p in pairs}
     key_high, key_low, key_right = {}, {}, {}
@@ -558,36 +528,36 @@
             right[h] = jnp.concatenate(
                 [conv(lin_v, spread_v, rim_v, conv_v, h), carried[h] * keys[p]], axis=1
             )
-    for h in range(heads):
-        solved[h] = (right[h] + mm(corrector[h], right[h].astype(BF))).astype(BF)
-    for h in range(heads):
-        right[h] = (
-            right[h]
-            - solved[h].astype(F32)
-            - mm(split_lower[h], jnp.concatenate([solved[h], solved[h]], axis=0))
-        )
-    for h in range(heads):
-        refined[h] = (right[h] + mm(corrector[h], right[h].astype(BF))).astype(BF)
-    for p in pairs:
-        parts = [
-            closing[h] * (solved[h][:, :DV].astype(F32) + refined[h][:, :DV].astype(F32))
-            for h in (2 * p, 2 * p + 1)
-        ]
-        wide = jnp.concatenate(parts, axis=1).astype(BF)
-        high, low = halves(keys[p].T)
-        made = mm(
-            jnp.concatenate([high, low], axis=1), jnp.concatenate([wide, wide], axis=0)
-        ).astype(BF)
-        state_out[2 * p] = made[:, :DV]
-        state_out[2 * p + 1] = made[:, DV:]
-
-    @pl.when(index < count - 1)
-    def _():
-        states.start()
-
-    arrived(early[3])
-    for name in ("taps_q", "q", "query", "gate", "z"):
-        loads[name].wait()
+    for g in range(GROUPS):
+        members = range(g * per_group, (g + 1) * per_group)
+        for h in members:
+            solved[h] = (right[h] + mm(corrector[h], right[h].astype(BF))).astype(BF)
+        for h in members:
+            right[h] = (
+                right[h]
+                - solved[h].astype(F32)
+                - mm(split_lower[h], jnp.concatenate([solved[h], solved[h]], axis=0))
+            )
+        for h in members:
+            refined[h] = (right[h] + mm(corrector[h], right[h].astype(BF))).astype(BF)
+        for p in pairs[g * per_group // 2 : (g + 1) * per_group // 2]:
+            parts = [
+                closing[h] * (solved[h][:, :DV].astype(F32) + refined[h][:, :DV].astype(F32))
+                for h in (2 * p, 2 * p + 1)
+            ]
+            wide = jnp.concatenate(parts, axis=1).astype(BF)
+            high, low = halves(keys[p].T)
+            made = mm(
+                jnp.concatenate([high, low], axis=1), jnp.concatenate([wide, wide], axis=0)
+            ).astype(BF)
+            state_out[2 * p] = made[:, :DV]
+            state_out[2 * p + 1] = made[:, DV:]
+
+        @pl.when(index < count - 1)
+        def _(g=g):
+            states[g].start()
+
+    arrived(early[2], early[3])
 
     for p in pairs:
         query = unit(conv(lin_q, spread_q, rim_q, conv_q, p)) * DK ** (-0.5)
@@ -621,8 +591,9 @@
         gate = lin_z[:, pl.ds(h * DV, DV)].astype(F32)
         gates[h] = gate / (1.0 + jnp.exp(-gate))
 
-    arrived(states)
     for h in range(heads):
+        if h % per_group == 0:
+            arrived(states[h // per_group])
         state = state_in[h]
         value = local_out[h] + mm(reach_out[h], jnp.concatenate([state, state], axis=0))
         scale = lax.rsqrt(jnp.mean(value * value, axis=1, keepdims=True) + 1e-06)
@@ -630,7 +601,7 @@
 
     @pl.when(index < count - 1)
     def _():
-        for copy in early + [states]:
+        for copy in early + states:
             copy.wait_send()
 
 
@@ -669,18 +640,16 @@
         attn_gate,
     )
     vmem = pl.BlockSpec(memory_space=pltpu.VMEM)
-    rim = 16
+    rim = 8
     return pl.pallas_call(
         functools.partial(fused_kernel, lax.axis_size("seq")),
         out_shape=(
             jax.ShapeDtypeStruct(lin_z.shape, BF),
             jax.ShapeDtypeStruct(attn_query.shape, BF),
         ),
-        in_specs=[pl.BlockSpec(memory_space=pltpu.SMEM), vmem]
-        + [pl.BlockSpec(memory_space=pltpu.HBM)] * len(streamed),
+        in_specs=[pl.BlockSpec(memory_space=pltpu.SMEM)] + [vmem] * 12,
         out_specs=(vmem, vmem),
-        scratch_shapes=[pltpu.VMEM(x.shape, x.dtype) for x in streamed]
-        + [
+        scratch_shapes=[
             pltpu.VMEM((rim, lin_q.shape[1]), BF),
             pltpu.VMEM((rim, lin_k.shape[1]), BF),
             pltpu.VMEM((rim, lin_v.shape[1]), BF),
@@ -693,9 +662,8 @@
             pltpu.VMEM((heads, rows, DV), F32),
             pltpu.VMEM((heads, rows, 2 * DK), BF),
             pltpu.VMEM((heads, rows, DV), F32),
-            pltpu.SemaphoreType.DMA((5,)),
-            pltpu.SemaphoreType.DMA((5,)),
-            pltpu.SemaphoreType.DMA((len(streamed),)),
+            pltpu.SemaphoreType.DMA((4 + GROUPS,)),
+            pltpu.SemaphoreType.DMA((4 + GROUPS,)),
         ],
         compiler_params=pltpu.CompilerParams(
             collective_id=0, has_side_effects=True, vmem_limit_bytes=48 * 1024 * 1024

time: 19.7 us -> 19.4 us (0.985)
  Pallas kernels: 14.1 us -> 13.8 us
    pallas_call x1, Pallas kernels: 14.1 us -> 13.8 us  [fused(): pl.pallas_call(functools.partial(fused_kernel, lax.axis_size('seq')), out...]
where the time goes in v4:
time: 19.4 us; the launch traced here: 19.2 us
  Pallas kernels  13.8 us (71%)
  local copies, waits for them, and re-layouts  4.6 us (24%)
  between operations  0.79 us (4%)
    pallas_call x1, Pallas kernels, fused(): pl.pallas_call(functools.partial(fused_kernel, lax.axis_size('seq')), out...  13.8 us
    unnamed x29, local copies, waits for them, and re-layouts  4.21 us

profile of v4, /device:TPU:18, one launch (start us, length us, event | category | flops | bytes accessed | tf_op | source)
XLA Modules:
  0.0 19.2 jit_solution(3527311975709682940)
XLA Ops:
  0.6 0.0 copy-start
  0.7 0.0 copy-start.9
  0.7 0.0 copy-start.10
  0.7 0.0 copy-start.11
  0.7 0.0 copy-start.7
  0.7 0.0 copy-start.8
  0.7 0.9 %copy-done = bf16[128,2,2,256]{3,2,1,0:T(2,128)(2,1)S(1)} copy-done((bf16[128,2,2,256]{3,2,1,0:T(2,128)(2,1)S(1)}, bf16[128,2,2,256]{3,2,1,0:T(2,128)(2,1)}, u32[]{:S(2)}) %copy-start) | copy-done | bytes 262168
  1.6 0.3 %constant_dynamic-slice_fusion = bf16[128,2,1,256]{3,2,1,0:T(2,128)(2,1)S(1)} fusion(bf16[128,2,2,256]{3,2,1,0:T(2,128)(2,1)S(1)} %copy-done, s32[]{:T(128)S(6)} %select_n.10), kind=kLoop, calls=%fused_computation | loop fusion | bytes 262148 | tf_op jit(solution)/shard_map/jit(dynamic_index_in_dim)/dynamic_slice | solution.py:627
  1.9 0.0 copy-start.1
  1.9 0.0 copy-start.2
  1.9 0.2 copy.17
  2.1 0.0 copy-start.5
  2.1 0.0 copy-start.12
  2.1 0.1 copy.16.kv_own
  2.2 0.0 copy-done.9
  2.3 0.3 %copy-done.3 = bf16[128,1024]{1,0:T(8,128)(2,1)S(1)} copy-done((bf16[128,1024]{1,0:T(8,128)(2,1)S(1)}, bf16[128,1024]{1,0:T(8,128)(2,1)}, u32[]{:S(2)}) %copy-start.3) | copy-done | bytes 262168
  2.5 0.1 copy-done.4
  2.6 0.2 %copy-done.1 = bf16[128,1024]{1,0:T(8,128)(2,1)S(1)} copy-done((bf16[128,1024]{1,0:T(8,128)(2,1)S(1)}, bf16[128,1024]{1,0:T(8,128)(2,1)}, u32[]{:S(2)}) %copy-start.1) | copy-done | bytes 262168
  2.9 0.1 copy-done.2
  2.9 0.1 copy-done.5
  3.1 0.9 %copy-done.6 = bf16[128,512]{1,0:T(8,128)(2,1)S(1)} copy-done((bf16[128,512]{1,0:T(8,128)(2,1)S(1)}, bf16[128,512]{1,0:T(8,128)(2,1)}, u32[]{:S(2)}) %copy-start.6) | copy-done | bytes 131096
  4.0 13.8 %shard_map.140 = (bf16[128,1024]{1,0:T(8,128)(2,1)S(1)}, bf16[128,1024]{1,0:T(8,128)(2,1)S(1)}) custom-call(s32[5]{0:T(128)S(1)} %copy-done.12, bf16[128,512]{1,0:T(8,128)(2,1)S(1)} %copy.16.kv_own, bf16[128,512]{1,0:T(8,128)(2,1)S(1)} %copy-done.5, bf16[128,512]{1,0:T(8,128)(2,1)S(1)} %copy-done.6, bf16[128,1024]{1,0:T(8,128)(2,1)S(1)} %copy-done.1, ...), custom_call_target="tpu_custom_call" | custom-call | tf_op jit(solution)/shard_map/pallas_call | solution.py:644
  17.8 0.7 %copy.20 = bf16[128,1024]{1,0:T(8,128)(2,1)} copy(bf16[128,1024]{1,0:T(8,128)(2,1)S(1)} %get-tuple-element.4) | data formatting | bytes 524288
  18.5 0.7 %copy.21 = bf16[128,1024]{1,0:T(8,128)(2,1)} copy(bf16[128,1024]{1,0:T(8,128)(2,1)S(1)} %get-tuple-element.5) | data formatting | bytes 524288
  (8 shorter events, 0.0 us)
Async XLA Ops:
  0.6 1.0 %copy-start = (bf16[128,2,2,256]{3,2,1,0:T(2,128)(2,1)S(1)}, bf16[128,2,2,256]{3,2,1,0:T(2,128)(2,1)}, u32[]{:S(2)}) copy-start(bf16[128,2,2,256]{3,2,1,0:T(2,128)(2,1)} %param.24) | copy-start | bytes 786436
  0.7 1.6 %copy-start.9 = (bf16[4,512]{1,0:T(4,128)(2,1)S(1)}, bf16[4,512]{1,0:T(4,128)(2,1)}, u32[]{:S(2)}) copy-start(bf16[4,512]{1,0:T(4,128)(2,1)} %conv_k.1) | copy-start | bytes 12292
  0.7 1.6 %copy-start.10 = (f32[128,8]{0,1:T(8,128)S(1)}, f32[128,8]{0,1:T(8,128)}, u32[]{:S(2)}) copy-start(f32[128,8]{0,1:T(8,128)} %param.20) | copy-start | bytes 12292
  0.7 1.6 %copy-start.11 = (f32[128,8]{0,1:T(8,128)S(1)}, f32[128,8]{0,1:T(8,128)}, u32[]{:S(2)}) copy-start(f32[128,8]{0,1:T(8,128)} %param.21) | copy-start | bytes 12292
  0.7 1.6 %copy-start.7 = (bf16[4,1024]{1,0:T(4,128)(2,1)S(1)}, bf16[4,1024]{1,0:T(4,128)(2,1)}, u32[]{:S(2)}) copy-start(bf16[4,1024]{1,0:T(4,128)(2,1)} %conv_v.1) | copy-start | bytes 24580
  0.7 1.6 %copy-start.8 = (bf16[4,512]{1,0:T(4,128)(2,1)S(1)}, bf16[4,512]{1,0:T(4,128)(2,1)}, u32[]{:S(2)}) copy-start(bf16[4,512]{1,0:T(4,128)(2,1)} %conv_q.1) | copy-start | bytes 12292
  1.6 0.9 %copy-start.3 = (bf16[128,1024]{1,0:T(8,128)(2,1)S(1)}, bf16[128,1024]{1,0:T(8,128)(2,1)}, u32[]{:S(2)}) copy-start(bf16[128,1024]{1,0:T(8,128)(2,1)} %attn_query.1) | copy-start | bytes 786436
  1.6 1.0 %copy-start.4 = (bf16[128,1024]{1,0:T(8,128)(2,1)S(1)}, bf16[128,1024]{1,0:T(8,128)(2,1)}, u32[]{:S(2)}) copy-start(bf16[128,1024]{1,0:T(8,128)(2,1)} %attn_gate.1) | copy-start | bytes 786436
  1.9 1.0 %copy-start.1 = (bf16[128,1024]{1,0:T(8,128)(2,1)S(1)}, bf16[128,1024]{1,0:T(8,128)(2,1)}, u32[]{:S(2)}) copy-start(bf16[128,1024]{1,0:T(8,128)(2,1)} %lin_v.1) | copy-start | bytes 786436
  1.9 1.1 %copy-start.2 = (bf16[128,1024]{1,0:T(8,128)(2,1)S(1)}, bf16[128,1024]{1,0:T(8,128)(2,1)}, u32[]{:S(2)}) copy-start(bf16[128,1024]{1,0:T(8,128)(2,1)} %lin_z.1) | copy-start | bytes 786436
  2.1 1.0 %copy-start.5 = (bf16[128,512]{1,0:T(8,128)(2,1)S(1)}, bf16[128,512]{1,0:T(8,128)(2,1)}, u32[]{:S(2)}) copy-start(bf16[128,512]{1,0:T(8,128)(2,1)} %lin_q.1) | copy-start | bytes 393220
  2.1 1.0 %copy-start.12 = (s32[5]{0:T(128)S(1)}, s32[5]{0:T(128)}, u32[]{:S(2)}) copy-start(s32[5]{0:T(128)} %doc_ref.1) | copy-start | bytes 64
  3.1 0.9 %copy-start.6 = (bf16[128,512]{1,0:T(8,128)(2,1)S(1)}, bf16[128,512]{1,0:T(8,128)(2,1)}, u32[]{:S(2)}) copy-start(bf16[128,512]{1,0:T(8,128)(2,1)} %lin_k.1) | copy-start | bytes 393220
